TPU v7x, 128 devices: a whole 4x4x4 slice. The times are simulated.
128 devices in a mesh: seq: 16 (over y_hi, z, core), head: 8 (over x, y_lo).
Axes of the slice: x: 4, y: 4 (y_hi: 2, y_lo: 2; y = y_hi * 2 + y_lo), z: 4, core: 2. Of those that a mesh axis runs over, the one named last changes fastest.
Arguments:
- attn_query: bfloat16 [32768, 5120], P('seq', 'head'), may hold values from -45 to 45
- attn_key: bfloat16 [32768, 5120], P('seq', 'head'), may hold values from -15 to 15
- attn_value: bfloat16 [32768, 5120], P('seq', 'head'), may hold values from -6 to 6
- fast_query: bfloat16 [32768, 5120], P('seq', 'head'), may hold values from -6 to 6
- fast_key: bfloat16 [32768, 5120], P('seq', 'head'), may hold values from -6 to 6
- fast_value: bfloat16 [32768, 5120], P('seq', 'head'), may hold values from -6 to 6
- rates: float32 [32768, 8], P('seq', 'head'), may hold values from 0.00015625 to 0.0015625
- fast_weights: float32 [8, 640, 3, 640], P('head'), may hold values from -0.25 to 0.25
- gain: float32 [8, 640], P('head'), may hold values from 0.5 to 1.5
Outputs:
- mixed: bfloat16 [32768, 5120], P('seq', 'head')
- final_weights: float32 [8, 640, 3, 640], P('head', 'seq')
All inputs are finite; a program needn't handle non-finite values.
Results may differ from a plain program's by a relative error of at most 0.013.
Values may be sent and summed in bfloat16 or wider, within the bound.
No kernel may reach another device: no remote copies, remote signals or barrier semaphores. Data moves between devices by JAX's collectives and lax.ppermute only.
A program may use at most 192 MiB of HBM per device.

v0:
```python
import math
from functools import partial

import jax
import jax.numpy as jnp
from jax import lax
from jax.experimental import pallas as pl
from jax.experimental.pallas import tpu as pltpu
from jax.sharding import PartitionSpec as P

AH = 128
WINDOW = 512
SUB = 256
EPSILON = 1e-06
F32 = jnp.float32
BF16 = jnp.bfloat16


def dot(a, b, contract):
    return lax.dot_general(a, b, (contract, ((), ())), preferred_element_type=F32)


NT = ((1,), (1,))
NN = ((1,), (0,))


def params(mib=40):
    return pltpu.CompilerParams(
        dimension_semantics=("arbitrary",), vmem_limit_bytes=mib << 20
    )


def attention_body(first, info_ref, q_ref, kp_ref, kc_ref, vp_ref, vc_ref, o_ref):
    heads = q_ref.shape[1] // AH
    scale = math.log2(math.e) / math.sqrt(AH)
    row = lax.broadcasted_iota(jnp.int32, (SUB, SUB), 0)
    col = lax.broadcasted_iota(jnp.int32, (SUB, SUB), 1)
    older = col > row
    ones = jnp.ones((SUB, AH), BF16)
    bias = jnp.where(info_ref[0] == 0, -1e30, 0.0).astype(F32) if first else None
    for h in range(heads):
        cols = slice(h * AH, (h + 1) * AH)
        keys = [kp_ref[:SUB, cols], kp_ref[SUB:, cols], kc_ref[:SUB, cols], kc_ref[SUB:, cols]]
        values = [
            jnp.concatenate([v, ones], 1)
            for v in (vp_ref[:SUB, cols], vp_ref[SUB:, cols], vc_ref[:SUB, cols], vc_ref[SUB:, cols])
        ]
        for strip in range(2):
            q = q_ref[strip * SUB : (strip + 1) * SUB, cols]
            old, mid, new = (dot(q, keys[strip + n], NT) for n in range(3))
            if first:
                old = old + bias
                if strip == 0:
                    mid = mid + bias
            edge = jnp.where(older, old, new)
            top = jnp.max(jnp.maximum(edge, mid), axis=1, keepdims=True)
            edge = jnp.exp2((edge - top) * scale)
            mid = jnp.exp2((mid - top) * scale).astype(BF16)
            old = jnp.where(older, edge, 0.0).astype(BF16)
            new = jnp.where(older, 0.0, edge).astype(BF16)
            out = (
                dot(old, values[strip], NN)
                + dot(mid, values[strip + 1], NN)
                + dot(new, values[strip + 2], NN)
            )
            o_ref[strip * SUB : (strip + 1) * SUB, cols] = out[:, :AH] / out[:, AH:]


def attention_first(info, q, k, v, halo_k, halo_v, partly):
    rows, width = q.shape
    tile = pl.BlockSpec((WINDOW, width), lambda i, s: (0, 0))

    def body(info_ref, q_ref, kp_ref, kc_ref, vp_ref, vc_ref, _, o_ref):
        attention_body(True, info_ref, q_ref, kp_ref, kc_ref, vp_ref, vc_ref, o_ref)

    return pl.pallas_call(
        body,
        out_shape=jax.ShapeDtypeStruct((rows, width), F32),
        grid_spec=pltpu.PrefetchScalarGridSpec(
            num_scalar_prefetch=1,
            grid=(1,),
            in_specs=[tile] * 5 + [pl.BlockSpec(memory_space=pl.ANY)],
            out_specs=tile,
        ),
        input_output_aliases={6: 0},
        compiler_params=params(),
        name="attention_first",
    )(info, q, halo_k, k, halo_v, v, partly)


def attention_rest(info, q, k, v, block, partly=None):
    rows, width = q.shape

    def at(offset):
        return pl.BlockSpec(
            (WINDOW, width), lambda i, s: (jnp.where(s[1] == block, i, 0) + offset, 0)
        )

    def body(info_ref, q_ref, kp_ref, kc_ref, vp_ref, vc_ref, *rest):
        @pl.when(info_ref[1] == block)
        def _():
            attention_body(False, info_ref, q_ref, kp_ref, kc_ref, vp_ref, vc_ref, rest[-1])

        if partly is not None:

            @pl.when(info_ref[1] != block)
            def _():
                rest[-1][...] = rest[0][...]

    kept = [] if partly is None else [partly]
    return pl.pallas_call(
        body,
        out_shape=jax.ShapeDtypeStruct((rows, width), F32),
        grid_spec=pltpu.PrefetchScalarGridSpec(
            num_scalar_prefetch=1,
            grid=(rows // WINDOW - 1,),
            in_specs=[at(1), at(0), at(1), at(0), at(1)]
            + [pl.BlockSpec((WINDOW, width), lambda i, s: (1, 0)) for _ in kept],
            out_specs=at(1),
        ),
        input_output_aliases={6: 0} if kept else {},
        compiler_params=params(),
        name=f"attention_rest_{block}",
    )(info, q, k, k, v, v, *kept)


SLOTS = 8
RING = 4


class Chunk:
    def __init__(self, name, spans):
        self.name = name
        self.spans = spans
        self.span = sum(n for _, _, n in spans)
        self.rows = SLOTS * self.span


EARLY = Chunk("early", ((0, 0, 40), (1, 0, 8)))
LATE = Chunk("late", ((1, 8, 32),))
CHUNKS = (EARLY, LATE)


def factors(chunk, base, w_ref, keys_ref, values_ref, rate_ref, x_ref, at):
    n = chunk.rows
    keys = keys_ref[at]
    values = values_ref[at]
    rate = rate_ref[:, at]
    gate_pre = dot(w_ref[:n], keys, NT)
    up_pre = dot(w_ref[n : 2 * n], keys, NT)
    back = dot(w_ref[2 * n :], values, NT) * rate
    sig = 0.5 * jnp.tanh(0.5 * gate_pre) + 0.5
    active = gate_pre * sig
    x_ref[0, base : base + n, at] = (back * up_pre * (sig + active * (1.0 - sig))).astype(BF16)
    x_ref[1, base : base + n, at] = (back * active).astype(BF16)
    x_ref[2, base : base + n, at] = (active * up_pre * rate).astype(BF16)


TILE = 512


class Tokens:
    def __init__(self, key_hbm, value_hbm, keys_ref, values_ref, sems):
        self.pairs = ((key_hbm, keys_ref), (value_hbm, values_ref))
        self.sems = sems
        self.count = keys_ref.shape[0] // TILE

    def at(self, t):
        return pl.ds(pl.multiple_of(t * TILE, TILE), TILE)

    def copies(self, t):
        return [
            pltpu.make_async_copy(hbm.at[self.at(t)], ref.at[self.at(t)], self.sems.at[n, t])
            for n, (hbm, ref) in enumerate(self.pairs)
        ]

    def start(self, t):
        for copy in self.copies(t):
            copy.start()

    def wait(self, t):
        for copy in self.copies(t):
            copy.wait()


def contract(x_ref, keys_ref, values_ref, outs):
    for m in range(3):
        right = (values_ref if m == 2 else keys_ref)[...]
        term = dot(x_ref[m], right, NN)
        base = 0
        for chunk, (mine_ref, theirs_ref) in zip(CHUNKS, outs):
            span = chunk.span
            for d in range(RING):
                for e, ref in enumerate((mine_ref, theirs_ref)):
                    at = base + span * (2 * d + e)
                    ref[d, m * span : (m + 1) * span] = term[at : at + span].astype(BF16)
            base += chunk.rows


def row_copies(chunk, info_ref, fw_hbm, rows_ref, sems):
    half = fw_hbm.shape[1] // 2
    owned = half // SLOTS
    z, c = info_ref[2], info_ref[3]
    copies = []
    for d in range(RING):
        for e in range(2):
            owner = 2 * lax.rem(z + d, RING) + (c if e == 0 else 1 - c)
            at = (2 * d + e) * chunk.span
            for h, lo, n in chunk.spans:
                start = pl.multiple_of(owner * owned + h * half + lo, 8)
                copies.append(
                    pltpu.make_async_copy(
                        fw_hbm.at[:, pl.ds(start, n)],
                        rows_ref.at[:, pl.ds(at, n)],
                        sems.at[len(copies)],
                    )
                )
                at += n
    return copies


def fill_gathered(chunk, base, sources, w_ref):
    for d in range(RING):
        for e in range(2):
            from_there = (-d) % RING
            ref = sources[RING].at[from_there] if e else sources[from_there]
            for m in range(3):
                at = (m * SLOTS + 2 * d + e) * chunk.span
                here = base + m * chunk.span
                w_ref[at : at + chunk.span] = ref[here : here + chunk.span]


HERE = pl.BlockSpec(memory_space=pltpu.VMEM)
ANYWHERE = pl.BlockSpec(memory_space=pl.ANY)


SPLIT = 3 * EARLY.span
PIECE = SPLIT + 3 * LATE.span


def gradient_shapes(rows, width, chunked):
    heights = (SPLIT, PIECE - SPLIT) if chunked else (PIECE,)
    pieces = [
        jax.ShapeDtypeStruct((RING, height, width), BF16) for height in heights for _ in range(2)
    ]
    scratch = [pltpu.VMEM((3 * chunk.rows, width), BF16) for chunk in CHUNKS] + [
        pltpu.VMEM((3, sum(chunk.rows for chunk in CHUNKS), rows), BF16),
        pltpu.VMEM((rows, width), BF16),
        pltpu.VMEM((rows, width), BF16),
        pltpu.SemaphoreType.DMA((2,)),
        pltpu.SemaphoreType.DMA((2, rows // TILE)),
    ]
    return pieces, scratch


def gradient_first(info, initial, keys, values, rates):
    rows, width = keys.shape
    pieces, scratch = gradient_shapes(rows, width, False)
    weights = [jax.ShapeDtypeStruct((3 * chunk.rows, width), BF16) for chunk in CHUNKS]

    def body(info_ref, fw_hbm, key_hbm, value_hbm, rate_ref, mine, theirs, *refs):
        outs, held, refs = refs[:2], refs[2:4], refs[4:]
        x_ref, ks_ref, vs_ref, w_sems, t_sems, *refs = refs
        raw, row_sems = refs[:2], refs[2:]

        @pl.when(info_ref[1] == 0)
        def _():
            tokens = Tokens(key_hbm, value_hbm, ks_ref, vs_ref, t_sems)
            fetches = [
                row_copies(chunk, info_ref, fw_hbm, ref, sems)
                for chunk, ref, sems in zip(CHUNKS, raw, row_sems)
            ]
            saves = [pltpu.make_async_copy(held[i], outs[i], w_sems.at[i]) for i in range(2)]

            def part(i, t):
                base = i * EARLY.rows
                factors(CHUNKS[i], base, held[i], ks_ref, vs_ref, rate_ref, x_ref, tokens.at(t))

            for copy in fetches[0]:
                copy.start()
            tokens.start(0)
            for i, chunk in enumerate(CHUNKS):
                for copy in fetches[i]:
                    copy.wait()
                if i == 0:
                    for copy in fetches[1]:
                        copy.start()
                    tokens.start(1)
                for m in range(3):
                    held[i][m * chunk.rows : (m + 1) * chunk.rows] = raw[i][m].astype(BF16)
                if i == 0:
                    tokens.wait(0)
                part(i, 0)

            def one_tile(t, carry):
                @pl.when(t + 1 < tokens.count)
                def _():
                    tokens.start(t + 1)

                tokens.wait(t)
                part(0, t)
                part(1, t)
                return carry

            lax.fori_loop(1, tokens.count, one_tile, 0)
            for save in saves:
                save.start()
            halves = [
                [ref.at[:, at] for ref in (mine, theirs)]
                for at in (slice(0, SPLIT), slice(SPLIT, PIECE))
            ]
            contract(x_ref, ks_ref, vs_ref, halves)
            for save in saves:
                save.wait()

    return pl.pallas_call(
        body,
        out_shape=pieces + weights,
        grid_spec=pltpu.PrefetchScalarGridSpec(
            num_scalar_prefetch=1,
            grid=(1,),
            in_specs=[ANYWHERE] * 3 + [pl.BlockSpec(rates.shape, lambda i, s: (0, 0))],
            out_specs=[HERE] * 2 + [ANYWHERE] * 2,
            scratch_shapes=scratch
            + [pltpu.VMEM((3, chunk.rows, width), F32) for chunk in CHUNKS]
            + [pltpu.SemaphoreType.DMA((SLOTS * len(chunk.spans),)) for chunk in CHUNKS],
        ),
        compiler_params=params(),
        name="gradient_first",
    )(info, initial, keys, values, rates)


def gradient_second(info, gathered, keys, values, rates, kept):
    rows, width = keys.shape
    pieces, scratch = gradient_shapes(rows, width, True)
    count = RING + 1

    def body(info_ref, *refs):
        sources, refs = refs[:count], refs[count:]
        key_hbm, value_hbm, rate_ref, _, _, ma, ta, mb, tb, *refs = refs
        outs, held, refs = refs[:2], refs[2:4], refs[4:]
        x_ref, ks_ref, vs_ref, w_sems, t_sems = refs

        @pl.when(info_ref[1] == 1)
        def _():
            tokens = Tokens(key_hbm, value_hbm, ks_ref, vs_ref, t_sems)
            tokens.start(0)
            saves = [pltpu.make_async_copy(held[i], outs[i], w_sems.at[i]) for i in range(2)]
            for i, chunk in enumerate(CHUNKS):
                fill_gathered(chunk, i * SPLIT, sources, held[i])

            def one_tile(t, carry):
                @pl.when(t + 1 < tokens.count)
                def _():
                    tokens.start(t + 1)

                tokens.wait(t)
                for i, chunk in enumerate(CHUNKS):
                    base = i * EARLY.rows
                    factors(chunk, base, held[i], ks_ref, vs_ref, rate_ref, x_ref, tokens.at(t))
                return carry

            lax.fori_loop(0, tokens.count, one_tile, 0)
            for save in saves:
                save.start()
            contract(x_ref, ks_ref, vs_ref, ((ma, ta), (mb, tb)))
            for save in saves:
                save.wait()

    return pl.pallas_call(
        body,
        out_shape=pieces + [jax.ShapeDtypeStruct(w.shape, BF16) for w in kept],
        grid_spec=pltpu.PrefetchScalarGridSpec(
            num_scalar_prefetch=1,
            grid=(1,),
            in_specs=[HERE] * count
            + [ANYWHERE] * 2
            + [pl.BlockSpec(rates.shape, lambda i, s: (0, 0))]
            + [ANYWHERE] * 2,
            out_specs=[HERE] * 4 + [ANYWHERE] * 2,
            scratch_shapes=scratch,
        ),
        input_output_aliases={count + 4: 4, count + 5: 5},
        compiler_params=params(),
        name="gradient_second",
    )(info, *gathered, keys, values, rates, *kept)


def partial_output(q, w_ref):
    n = w_ref.shape[0] // 3
    gate_pre = dot(q, w_ref[:n], NT)
    up_pre = dot(q, w_ref[n : 2 * n], NT)
    sig = 0.5 * jnp.tanh(0.5 * gate_pre) + 0.5
    return dot((gate_pre * sig * up_pre).astype(BF16), w_ref[2 * n :], NN)


def fast_apply(info, queries, weights, gain, attended, tiles, partly=None, tile=512):
    rows, width = queries.shape
    stream = pl.BlockSpec((tile, width), lambda i, s: (i + tiles[0], 0))
    kept = [] if partly is None else [partly]

    def body(info_ref, q_ref, early_ref, late_ref, gain_ref, att_ref, *rest):
        q = q_ref[...]
        out = partial_output(q, early_ref) + partial_output(q, late_ref)
        inverse_rms = lax.rsqrt(jnp.mean(out * out, axis=-1, keepdims=True) + EPSILON)
        rest[-1][...] = (att_ref[...] + out * inverse_rms * gain_ref[...]).astype(BF16)

    return pl.pallas_call(
        body,
        out_shape=jax.ShapeDtypeStruct((rows, width), BF16),
        grid_spec=pltpu.PrefetchScalarGridSpec(
            num_scalar_prefetch=1,
            grid=(tiles[1] - tiles[0],),
            in_specs=[stream]
            + [
                pl.BlockSpec(w.shape, lambda i, s: (0, 0), pipeline_mode=pl.Buffered(1))
                for w in weights
            ]
            + [pl.BlockSpec((1, width), lambda i, s: (0, 0)), stream]
            + [ANYWHERE for _ in kept],
            out_specs=stream,
        ),
        input_output_aliases={6: 0} if kept else {},
        compiler_params=params(32),
        name=f"fast_apply_{tiles[0]}",
    )(info, queries, *weights, gain, attended, *kept)


def renormalize(previous, gradient):
    moved = previous + gradient
    size = jnp.mean(previous * previous, axis=-1, keepdims=True) + EPSILON
    moved_size = jnp.mean(moved * moved, axis=-1, keepdims=True) + EPSILON
    return moved * (jnp.sqrt(size) / jnp.sqrt(moved_size))


def total(mine_ref, other_ref, *arrived):
    out = mine_ref[0].astype(F32) + other_ref[0].astype(F32)
    for ref in arrived:
        out = out + ref[...].astype(F32)
    return out


def middle_call(info, mine, other, arrived, fast_weights):
    _, height, width = mine.shape
    owned = fast_weights.shape[1] // (2 * SLOTS)

    def half(h):
        return pl.BlockSpec(
            (3, owned, width), lambda i, s: (0, h * SLOTS + 2 * s[2] + s[3], 0)
        )

    def body(info_ref, mine_ref, other_ref, a_ref, b_ref, c_ref, w0_ref, w1_ref, cast_ref, keep_ref):
        gradient = total(mine_ref, other_ref, a_ref, b_ref, c_ref)
        base = 0
        for chunk in CHUNKS:
            for m in range(3):
                old = [(w0_ref, w1_ref)[h][m, lo : lo + n] for h, lo, n in chunk.spans]
                here = slice(base, base + chunk.span)
                new = renormalize(jnp.concatenate(old, 0), gradient[here])
                cast_ref[here] = new.astype(BF16)
                if chunk is EARLY:
                    keep_ref[m] = new[:owned]
                base += chunk.span

    return pl.pallas_call(
        body,
        out_shape=(
            jax.ShapeDtypeStruct((height, width), BF16),
            jax.ShapeDtypeStruct((3, owned, width), F32),
        ),
        grid_spec=pltpu.PrefetchScalarGridSpec(
            num_scalar_prefetch=1,
            grid=(1,),
            in_specs=[HERE] * 5 + [half(0), half(1)],
            out_specs=[HERE] * 2,
        ),
        compiler_params=params(16),
        name="middle_rows",
    )(info, mine, other, *arrived, fast_weights, fast_weights)


def sum_body(mine_ref, other_ref, a_ref, b_ref, c_ref, near_ref, far_ref):
    gradient = total(mine_ref, other_ref, a_ref, b_ref, c_ref)
    owned, rest = near_ref.shape[1], far_ref.shape[1]
    for m in range(3):
        at = m * (owned + rest)
        near_ref[m] = gradient[at : at + owned].astype(BF16)
        far_ref[m] = gradient[at + owned : at + owned + rest]


def sum_call(mine, other, arrived):
    _, span3, width = mine.shape
    owned = EARLY.spans[0][2]
    return pl.pallas_call(
        sum_body,
        out_shape=(
            jax.ShapeDtypeStruct((3, owned, width), BF16),
            jax.ShapeDtypeStruct((3, span3 // 3 - owned, width), F32),
        ),
        in_specs=[HERE] * 5,
        out_specs=[HERE] * 2,
        compiler_params=pltpu.CompilerParams(vmem_limit_bytes=16 << 20),
        name="second_sum",
    )(mine, other, *arrived)


def final_far(info, mine, other, arrived, cast, far):
    shape = (3, EARLY.spans[0][2], cast.shape[1])

    def body(info_ref, mine_ref, other_ref, a_ref, b_ref, c_ref, cast_ref, far_ref, o_ref):
        rest = far_ref.shape[1]
        owned = EARLY.span - rest

        @pl.when(info_ref[1] == 1)
        def _():
            gradient = total(mine_ref, other_ref, a_ref, b_ref, c_ref)
            for m in range(3):
                at = m * EARLY.span
                early = cast_ref[at : at + EARLY.span].astype(F32)[owned:]
                o_ref[m, :rest] = renormalize(early, far_ref[m])
                at = m * LATE.span
                late = cast_ref[SPLIT + at : SPLIT + at + LATE.span].astype(F32)
                o_ref[m, rest:] = renormalize(late, gradient[at : at + LATE.span])

    return pl.pallas_call(
        body,
        out_shape=jax.ShapeDtypeStruct(shape, F32),
        grid_spec=pltpu.PrefetchScalarGridSpec(
            num_scalar_prefetch=1, grid=(1,), in_specs=[HERE] * 7, out_specs=HERE
        ),
        compiler_params=params(16),
        name="final_far",
    )(info, mine, other, *arrived, cast, far)


def final_near(info, middle, near, far_rows):
    def body(info_ref, middle_ref, near_ref, far_ref, o_ref):
        @pl.when(info_ref[1] == 0)
        def _():
            for m in range(3):
                o_ref[m] = renormalize(middle_ref[m], near_ref[m].astype(F32))

        @pl.when(info_ref[1] == 1)
        def _():
            o_ref[...] = far_ref[...]

    return pl.pallas_call(
        body,
        out_shape=jax.ShapeDtypeStruct(middle.shape, F32),
        grid_spec=pltpu.PrefetchScalarGridSpec(
            num_scalar_prefetch=1, grid=(1,), in_specs=[HERE] * 3, out_specs=HERE
        ),
        compiler_params=params(16),
        name="final_near",
    )(info, middle, near, far_rows)


def send(x, pairs):
    return lax.ppermute(x, "seq", pairs)


def along_z(d):
    return [
        (8 * b + 2 * z + c, 8 * b + 2 * ((z + d) % RING) + c)
        for b in range(2)
        for z in range(RING)
        for c in range(2)
    ]


SIBLING = [(k, k ^ 1) for k in range(16)]
ACROSS = [(k, k + 8) for k in range(8)]
BACK = [(k + 8, k) for k in range(8)]


def in_hbm(x):
    return pltpu.with_memory_space_constraint(x, pltpu.HBM)


def after(x, *others):
    return lax.optimization_barrier((x, *others))[0]


def joined(mine, other):
    return [
        (mine[d].astype(F32) + other[d].astype(F32)).astype(BF16) for d in range(1, RING)
    ]


def around(pieces):
    return [send(piece, along_z(d + 1)) for d, piece in enumerate(pieces)]


def shards(
    attn_query, attn_key, attn_value, fast_query, fast_key, fast_value, rates, fast_weights, gain
):
    row_count, width = attn_query.shape
    seq = lax.axis_index("seq").astype(jnp.int32)
    info = jnp.stack([seq, seq // 8, (seq % 8) // 2, seq % 2])
    initial = in_hbm(jnp.transpose(fast_weights[0], (1, 0, 2)))
    tokens = (in_hbm(fast_key), in_hbm(fast_value), in_hbm(rates.reshape(1, row_count)))
    attn = tuple(in_hbm(x) for x in (attn_query, attn_key, attn_value))

    onward = [(i, (i + 1) % 16) for i in range(16)]
    tails = [x[row_count - WINDOW :] for x in (attn_key, attn_value)]

    mine, theirs, *weights = gradient_first(after(info, *tails), initial, *tokens)
    halo = [send(tail, onward) for tail in tails]
    other = send(after(theirs, *halo), SIBLING)
    parts = joined(mine, other)
    ring = around(parts)
    attended = attention_rest(after(info, *parts), *attn, 1)
    cast, middle = middle_call(after(info, attended), mine, other, ring, initial)
    own = send(cast, ACROSS)
    attended = attention_rest(after(info, cast), *attn, 0, attended)

    own = after(own, attended)
    ring = around([own] * (RING - 1))
    attended = attention_first(after(info, own), *attn, *halo, attended)
    column = [own] + [after(piece, attended) for piece in ring]
    beside = send(jnp.stack(column), SIBLING)
    mine_a, theirs_a, mine_b, theirs_b, *weights = gradient_second(
        info, [*column, beside], *tokens, weights
    )
    other_a = send(theirs_a, SIBLING)
    other_b = send(theirs_b, SIBLING)
    part_a = joined(mine_a, other_a)
    ring_a = around(part_a)
    part_b = joined(after(mine_b, *part_a), other_b)
    apply = partial(fast_apply, queries=fast_query, weights=weights, gain=gain, attended=attended)
    mixed = apply(after(info, *part_b), tiles=(0, 3))
    near, far = sum_call(after(mine_a, mixed), other_a, ring_a)
    near = send(near, BACK)
    ring_b = around(part_b)
    mixed = apply(after(info, far), tiles=(3, 4), partly=mixed)
    far_rows = final_far(after(info, mixed), mine_b, other_b, ring_b, own, far)
    final = final_near(info, middle, near, far_rows)
    return mixed, jnp.transpose(final, (1, 0, 2))[None]


def solution(mesh):
    in_specs = (
        P("seq", "head"),
        P("seq", "head"),
        P("seq", "head"),
        P("seq", "head"),
        P("seq", "head"),
        P("seq", "head"),
        P("seq", "head"),
        P("head", None, None, None),
        P("head", None),
    )
    out_specs = (P("seq", "head"), P("head", "seq", None, None))
    return jax.shard_map(shards, mesh=mesh, in_specs=in_specs, out_specs=out_specs, check_vma=False)
```

profile of v0, /device:TPU:30, one launch (start us, length us, event | category | flops | bytes accessed | tf_op | source)
XLA Modules:
  0.0 124.9 jit_solution(13982088245668292798)
XLA Ops:
  3.0 2.1 %collective-permute-start = (bf16[512,640]{1,0:T(8,128)(2,1)S(1)}, bf16[512,640]{1,0:T(8,128)(2,1)S(1)}, u32[]{:S(2)}, u32[]{:S(2)}) collective-permute-start(bf16[512,640]{1,0:T(8,128)(2,1)S(1)} %slice.60), channel_id=1, source_target_pairs={{0,8},{8,16},{16,24},{24,32},{32,40},{40,48},{48,56},{56,64},{64,7... | collective-permute-start | bytes 1966088 | tf_op jit(solution)/shard_map/ppermute | solution.py:559
  5.2 1.5 %gradient_first.1 = (bf16[4,240,640]{2,1,0:T(8,128)(2,1)S(1)}, bf16[4,240,640]{2,1,0:T(8,128)(2,1)S(1)}, bf16[1152,640]{1,0:T(8,128)(2,1)S(1)}, bf16[768,640]{1,0:T(8,128)(2,1)S(1)}) custom-call(s32[4]{0:T(128)S(1)} %pad_add_fusion.info_ref, f32[3,640,640]{2,1,0:T(8,128)} %bitcast.37, bf16[2048,640]{1,0:T(8,128)(2,1)} %refs_5_.1, bf16[2048,640]{1,0:T(8,128)(2,1)} %refs_6_.1, ...), custom_call_target="tpu_custom_call" | custom-call | tf_op jit(solution)/shard_map/gradient_first/pallas_call | solution.py:316
  6.7 8.8 %collective-permute-done.1.vp_ref = bf16[512,640]{1,0:T(8,128)(2,1)S(1)} collective-permute-done((bf16[512,640]{1,0:T(8,128)(2,1)S(1)}, bf16[512,640]{1,0:T(8,128)(2,1)S(1)}, u32[]{:S(2)}, u32[]{:S(2)}) %collective-permute-start.1) | collective-permute-done | bytes 655392 | tf_op jit(solution)/shard_map/ppermute | solution.py:559
  15.5 7.0 %collective-permute-done.kp_ref = bf16[512,640]{1,0:T(8,128)(2,1)S(1)} collective-permute-done((bf16[512,640]{1,0:T(8,128)(2,1)S(1)}, bf16[512,640]{1,0:T(8,128)(2,1)S(1)}, u32[]{:S(2)}, u32[]{:S(2)}) %collective-permute-start) | collective-permute-done | bytes 655392 | tf_op jit(solution)/shard_map/ppermute | solution.py:559
  22.5 2.9 %collective-permute-done.2.other_ref = bf16[4,240,640]{2,1,0:T(8,128)(2,1)S(1)} collective-permute-done((bf16[4,240,640]{2,1,0:T(8,128)(2,1)S(1)}, bf16[4,240,640]{2,1,0:T(8,128)(2,1)S(1)}, u32[]{:S(2)}, u32[]{:S(2)}) %collective-permute-start.2) | collective-permute-done | bytes 1228832 | tf_op jit(solution)/shard_map/ppermute | solution.py:559
  26.2 1.6 %collective-permute-start.3 = (bf16[240,640]{1,0:T(8,128)(2,1)S(1)}, bf16[240,640]{1,0:T(8,128)(2,1)S(1)}, u32[]{:S(2)}, u32[]{:S(2)}) collective-permute-start(bf16[240,640]{1,0:T(8,128)(2,1)S(1)} %get-tuple-element.62), channel_id=1, source_target_pairs={{0,16},{8,24},{16,32},{24,40},{32,48},{40,56},{48,0},{56,8},{64,80... | collective-permute-start | bytes 921608 | tf_op jit(solution)/shard_map/ppermute | solution.py:559
  27.8 10.7 %attention_rest_1.1.rest_0_ = f32[2048,640]{1,0:T(8,128)S(1)} custom-call(s32[4]{0:T(128)S(1)} %pad_add_fusion.info_ref, bf16[2048,640]{1,0:T(8,128)(2,1)} %q_ref.7, bf16[2048,640]{1,0:T(8,128)(2,1)} %kc_ref.5, bf16[2048,640]{1,0:T(8,128)(2,1)} %kc_ref.5, bf16[2048,640]{1,0:T(8,128)(2,1)} %vc_ref.5, bf16[2048,640]{1,0:T(8,128)(2,1)} %vc_ref.5), custom_call_target="tpu_custom_call" | custom-call | tf_op jit(solution)/shard_map/attention_rest_1/pallas_call | solution.py:111
  38.5 4.8 %collective-permute-done.3.a_ref = bf16[240,640]{1,0:T(8,128)(2,1)S(1)} collective-permute-done((bf16[240,640]{1,0:T(8,128)(2,1)S(1)}, bf16[240,640]{1,0:T(8,128)(2,1)S(1)}, u32[]{:S(2)}, u32[]{:S(2)}) %collective-permute-start.3) | collective-permute-done | bytes 307232 | tf_op jit(solution)/shard_map/ppermute | solution.py:559
  43.3 2.0 %middle_rows.1 = (bf16[240,640]{1,0:T(8,128)(2,1)S(1)}, f32[3,40,640]{2,1,0:T(8,128)S(1)}) custom-call(s32[4]{0:T(128)S(1)} %pad_add_fusion.info_ref, bf16[4,240,640]{2,1,0:T(8,128)(2,1)S(1)} %get-tuple-element.32.mine_ref, bf16[4,240,640]{2,1,0:T(8,128)(2,1)S(1)} %collective-permute-done.2.other_ref, bf16[240,640]{1,0:T(8,128)(2,1)S(1)} %collective-permute-done.3.a_ref, ...), custom_call_target="tpu_custom_call" | custom-call | tf_op jit(solution)/shard_map/middle_rows/pallas_call | solution.py:465
  46.6 3.1 %attention_rest_0.1._ = f32[2048,640]{1,0:T(8,128)S(1)} custom-call(s32[4]{0:T(128)S(1)} %pad_add_fusion.info_ref, bf16[2048,640]{1,0:T(8,128)(2,1)} %q_ref.7, bf16[2048,640]{1,0:T(8,128)(2,1)} %kc_ref.5, bf16[2048,640]{1,0:T(8,128)(2,1)} %kc_ref.5, bf16[2048,640]{1,0:T(8,128)(2,1)} %vc_ref.5, ...), custom_call_target="tpu_custom_call", output_to_operand_aliasing={{}: (6, {})} | custom-call | tf_op jit(solution)/shard_map/attention_rest_0/pallas_call | solution.py:111
  49.7 9.6 %collective-permute-done.6.refs_0_.cast_ref = bf16[240,640]{1,0:T(8,128)(2,1)S(1)} collective-permute-done((bf16[240,640]{1,0:T(8,128)(2,1)S(1)}, bf16[240,640]{1,0:T(8,128)(2,1)S(1)}, u32[]{:S(2)}, u32[]{:S(2)}) %collective-permute-start.6) | collective-permute-done | bytes 307232 | tf_op jit(solution)/shard_map/ppermute | solution.py:559
  60.2 1.4 %collective-permute-start.7 = (bf16[240,640]{1,0:T(8,128)(2,1)S(1)}, bf16[240,640]{1,0:T(8,128)(2,1)S(1)}, u32[]{:S(2)}, u32[]{:S(2)}) collective-permute-start(bf16[240,640]{1,0:T(8,128)(2,1)S(1)} %collective-permute-done.6.refs_0_.cast_ref), channel_id=1, source_target_pairs={{0,16},{8,24},{16,32},{24,40},{32,48},{40,56},{48,0},{56,8},{64,80... | collective-permute-start | bytes 921608 | tf_op jit(solution)/shard_map/ppermute | solution.py:559
  61.7 4.6 %attention_first.1.att_ref = f32[2048,640]{1,0:T(8,128)S(1)} custom-call(s32[4]{0:T(128)S(1)} %pad_add_fusion.info_ref, bf16[2048,640]{1,0:T(8,128)(2,1)} %q_ref.7, bf16[512,640]{1,0:T(8,128)(2,1)S(1)} %collective-permute-done.kp_ref, bf16[2048,640]{1,0:T(8,128)(2,1)} %kc_ref.5, ...), custom_call_target="tpu_custom_call", output_to_operand_aliasing={{}: (6, {})} | custom-call | tf_op jit(solution)/shard_map/attention_first/pallas_call | solution.py:76
  66.2 3.3 %collective-permute-done.9.refs_3_ = bf16[240,640]{1,0:T(8,128)(2,1)S(1)} collective-permute-done((bf16[240,640]{1,0:T(8,128)(2,1)S(1)}, bf16[240,640]{1,0:T(8,128)(2,1)S(1)}, u32[]{:S(2)}, u32[]{:S(2)}) %collective-permute-start.9) | collective-permute-done | bytes 307232 | tf_op jit(solution)/shard_map/ppermute | solution.py:559
  69.5 1.6 %collective-permute-done.8.refs_2_ = bf16[240,640]{1,0:T(8,128)(2,1)S(1)} collective-permute-done((bf16[240,640]{1,0:T(8,128)(2,1)S(1)}, bf16[240,640]{1,0:T(8,128)(2,1)S(1)}, u32[]{:S(2)}, u32[]{:S(2)}) %collective-permute-start.8) | collective-permute-done | bytes 307232 | tf_op jit(solution)/shard_map/ppermute | solution.py:559
  71.1 5.0 %collective-permute-done.7.refs_1_ = bf16[240,640]{1,0:T(8,128)(2,1)S(1)} collective-permute-done((bf16[240,640]{1,0:T(8,128)(2,1)S(1)}, bf16[240,640]{1,0:T(8,128)(2,1)S(1)}, u32[]{:S(2)}, u32[]{:S(2)}) %collective-permute-start.7) | collective-permute-done | bytes 307232 | tf_op jit(solution)/shard_map/ppermute | solution.py:559
  76.4 2.9 %collective-permute-done.10.refs_4_ = bf16[4,240,640]{2,1,0:T(8,128)(2,1)S(1)} collective-permute-done((bf16[4,240,640]{2,1,0:T(8,128)(2,1)S(1)}, bf16[4,240,640]{2,1,0:T(8,128)(2,1)S(1)}, u32[]{:S(2)}, u32[]{:S(2)}) %collective-permute-start.10) | collective-permute-done | bytes 1228832 | tf_op jit(solution)/shard_map/ppermute | solution.py:559
  79.3 17.0 %gradient_second.1 = (bf16[4,144,640]{2,1,0:T(8,128)(2,1)S(1)}, bf16[4,144,640]{2,1,0:T(8,128)(2,1)S(1)}, bf16[4,96,640]{2,1,0:T(8,128)(2,1)S(1)}, bf16[4,96,640...) custom-call(s32[4]{0:T(128)S(1)} %pad_add_fusion.info_ref, ...), custom_call_target="tpu_custom_call", output_to_operand_aliasing={{4}: (9, {}), {5}: (10, {})} | custom-call | tf_op jit(solution)/shard_map/gradient_second/pallas_call | solution.py:370
  96.9 1.7 %collective-permute-done.11.other_ref = bf16[4,144,640]{2,1,0:T(8,128)(2,1)S(1)} collective-permute-done((bf16[4,144,640]{2,1,0:T(8,128)(2,1)S(1)}, bf16[4,144,640]{2,1,0:T(8,128)(2,1)S(1)}, u32[]{:S(2)}, u32[]{:S(2)}) %collective-permute-start.11) | collective-permute-done | bytes 737312 | tf_op jit(solution)/shard_map/ppermute | solution.py:559
  101.2 8.3 %fast_apply_0.1.rest_0_ = bf16[2048,640]{1,0:T(8,128)(2,1)} custom-call(s32[4]{0:T(128)S(1)} %pad_add_fusion.info_ref, bf16[2048,640]{1,0:T(8,128)(2,1)S(1)} %copy-done, bf16[1152,640]{1,0:T(8,128)(2,1)S(1)} %get-tuple-element.52.early_ref, bf16[768,640]{1,0:T(8,128)(2,1)S(1)} %get-tuple-element.53.late_ref, f32[1,640]{1,0:T(1,128)S(1)} %copy-done.1, ...), custom_call_target="tpu_custom_call" | custom-call | tf_op jit(solution)/shard_map/fast_apply_0/pallas_call | solution.py:408
  109.6 2.2 %collective-permute-done.13.a_ref = bf16[144,640]{1,0:T(8,128)(2,1)S(1)} collective-permute-done((bf16[144,640]{1,0:T(8,128)(2,1)S(1)}, bf16[144,640]{1,0:T(8,128)(2,1)S(1)}, u32[]{:S(2)}, u32[]{:S(2)}) %collective-permute-start.13) | collective-permute-done | bytes 184352 | tf_op jit(solution)/shard_map/ppermute | solution.py:559
  113.9 1.6 %collective-permute-start.18 = (bf16[96,640]{1,0:T(8,128)(2,1)S(1)}, bf16[96,640]{1,0:T(8,128)(2,1)S(1)}, u32[]{:S(2)}, u32[]{:S(2)}) collective-permute-start(bf16[96,640]{1,0:T(8,128)(2,1)S(1)} %get-tuple-element.67), channel_id=1, source_target_pairs={{0,32},{8,40},{16,48},{24,56},{32,0},{40,8},{48,16},{56,24},{64,96... | collective-permute-start | bytes 368648 | tf_op jit(solution)/shard_map/ppermute | solution.py:559
  116.3 3.7 %fast_apply_3.1 = bf16[2048,640]{1,0:T(8,128)(2,1)} custom-call(s32[4]{0:T(128)S(1)} %pad_add_fusion.info_ref, bf16[2048,640]{1,0:T(8,128)(2,1)S(1)} %copy-done, bf16[1152,640]{1,0:T(8,128)(2,1)S(1)} %get-tuple-element.52.early_ref, bf16[768,640]{1,0:T(8,128)(2,1)S(1)} %get-tuple-element.53.late_ref, ...), custom_call_target="tpu_custom_call", output_to_operand_aliasing={{}: (6, {})} | custom-call | tf_op jit(solution)/shard_map/fast_apply_3/pallas_call | solution.py:408
  121.2 1.6 %collective-permute-done.17.a_ref = bf16[96,640]{1,0:T(8,128)(2,1)S(1)} collective-permute-done((bf16[96,640]{1,0:T(8,128)(2,1)S(1)}, bf16[96,640]{1,0:T(8,128)(2,1)S(1)}, u32[]{:S(2)}, u32[]{:S(2)}) %collective-permute-start.17) | collective-permute-done | bytes 122912 | tf_op jit(solution)/shard_map/ppermute | solution.py:559
  (38 shorter events, 15.1 us)
Async XLA Ops:
  1.8 13.7 %collective-permute-start.1 = (bf16[512,640]{1,0:T(8,128)(2,1)S(1)}, bf16[512,640]{1,0:T(8,128)(2,1)S(1)}, u32[]{:S(2)}, u32[]{:S(2)}) collective-permute-start(bf16[512,640]{1,0:T(8,128)(2,1)S(1)} %slice.61), channel_id=1, source_target_pairs={{0,8},{8,16},{16,24},{24,32},{32,40},{40,48},{48,56},{56,64},{64,7... | collective-permute-start | bytes 1966088 | tf_op jit(solution)/shard_map/ppermute | solution.py:559
  3.0 19.5 %collective-permute-start = (bf16[512,640]{1,0:T(8,128)(2,1)S(1)}, bf16[512,640]{1,0:T(8,128)(2,1)S(1)}, u32[]{:S(2)}, u32[]{:S(2)}) collective-permute-start(bf16[512,640]{1,0:T(8,128)(2,1)S(1)} %slice.60), channel_id=1, source_target_pairs={{0,8},{8,16},{16,24},{24,32},{32,40},{40,48},{48,56},{56,64},{64,7... | collective-permute-start | bytes 1966088 | tf_op jit(solution)/shard_map/ppermute | solution.py:559
  22.5 2.9 %collective-permute-start.2 = (bf16[4,240,640]{2,1,0:T(8,128)(2,1)S(1)}, bf16[4,240,640]{2,1,0:T(8,128)(2,1)S(1)}, u32[]{:S(2)}, u32[]{:S(2)}) collective-permute-start(bf16[4,240,640]{2,1,0:T(8,128)(2,1)S(1)} %get-tuple-element.34), channel_id=1, source_target_pairs={{0,8},{8,0},{16,24},{24,16},{32,40},{40,32},{48,56},{56,48},{64,72... | collective-permute-start | bytes 3686408 | tf_op jit(solution)/shard_map/ppermute | solution.py:559
  25.7 12.8 %collective-permute-start.5 = (bf16[240,640]{1,0:T(8,128)(2,1)S(1)}, bf16[240,640]{1,0:T(8,128)(2,1)S(1)}, u32[]{:S(2)}, u32[]{:S(2)}) collective-permute-start(bf16[240,640]{1,0:T(8,128)(2,1)S(1)} %get-tuple-element.60), channel_id=1, source_target_pairs={{0,48},{8,56},{16,0},{24,8},{32,16},{40,24},{48,32},{56,40},{64,11... | collective-permute-start | bytes 921608 | tf_op jit(solution)/shard_map/ppermute | solution.py:559
  26.1 12.3 %collective-permute-start.4 = (bf16[240,640]{1,0:T(8,128)(2,1)S(1)}, bf16[240,640]{1,0:T(8,128)(2,1)S(1)}, u32[]{:S(2)}, u32[]{:S(2)}) collective-permute-start(bf16[240,640]{1,0:T(8,128)(2,1)S(1)} %get-tuple-element.61), channel_id=1, source_target_pairs={{0,32},{8,40},{16,48},{24,56},{32,0},{40,8},{48,16},{56,24},{64,96... | collective-permute-start | bytes 921608 | tf_op jit(solution)/shard_map/ppermute | solution.py:559
  26.2 17.1 %collective-permute-start.3 = (bf16[240,640]{1,0:T(8,128)(2,1)S(1)}, bf16[240,640]{1,0:T(8,128)(2,1)S(1)}, u32[]{:S(2)}, u32[]{:S(2)}) collective-permute-start(bf16[240,640]{1,0:T(8,128)(2,1)S(1)} %get-tuple-element.62), channel_id=1, source_target_pairs={{0,16},{8,24},{16,32},{24,40},{32,48},{40,56},{48,0},{56,8},{64,80... | collective-permute-start | bytes 921608 | tf_op jit(solution)/shard_map/ppermute | solution.py:559
  45.3 14.0 %collective-permute-start.6 = (bf16[240,640]{1,0:T(8,128)(2,1)S(1)}, bf16[240,640]{1,0:T(8,128)(2,1)S(1)}, u32[]{:S(2)}, u32[]{:S(2)}) collective-permute-start(bf16[240,640]{1,0:T(8,128)(2,1)S(1)} %get-tuple-element.37), channel_id=1, source_target_pairs={{0,64},{8,72},{16,80},{24,88},{32,96},{40,104},{48,112},{56,120},{... | collective-permute-start | bytes 921608 | tf_op jit(solution)/shard_map/ppermute | solution.py:559
  59.3 10.2 %collective-permute-start.9 = (bf16[240,640]{1,0:T(8,128)(2,1)S(1)}, bf16[240,640]{1,0:T(8,128)(2,1)S(1)}, u32[]{:S(2)}, u32[]{:S(2)}) collective-permute-start(bf16[240,640]{1,0:T(8,128)(2,1)S(1)} %collective-permute-done.6.refs_0_.cast_ref), channel_id=1, source_target_pairs={{0,48},{8,56},{16,0},{24,8},{32,16},{40,24},{48,32},{56,40},{64,11... | collective-permute-start | bytes 921608 | tf_op jit(solution)/shard_map/ppermute | solution.py:559
  59.3 11.8 %collective-permute-start.8 = (bf16[240,640]{1,0:T(8,128)(2,1)S(1)}, bf16[240,640]{1,0:T(8,128)(2,1)S(1)}, u32[]{:S(2)}, u32[]{:S(2)}) collective-permute-start(bf16[240,640]{1,0:T(8,128)(2,1)S(1)} %collective-permute-done.6.refs_0_.cast_ref), channel_id=1, source_target_pairs={{0,32},{8,40},{16,48},{24,56},{32,0},{40,8},{48,16},{56,24},{64,96... | collective-permute-start | bytes 921608 | tf_op jit(solution)/shard_map/ppermute | solution.py:559
  60.2 15.8 %collective-permute-start.7 = (bf16[240,640]{1,0:T(8,128)(2,1)S(1)}, bf16[240,640]{1,0:T(8,128)(2,1)S(1)}, u32[]{:S(2)}, u32[]{:S(2)}) collective-permute-start(bf16[240,640]{1,0:T(8,128)(2,1)S(1)} %collective-permute-done.6.refs_0_.cast_ref), channel_id=1, source_target_pairs={{0,16},{8,24},{16,32},{24,40},{32,48},{40,56},{48,0},{56,8},{64,80... | collective-permute-start | bytes 921608 | tf_op jit(solution)/shard_map/ppermute | solution.py:559
  76.3 3.0 %collective-permute-start.10 = (bf16[4,240,640]{2,1,0:T(8,128)(2,1)S(1)}, bf16[4,240,640]{2,1,0:T(8,128)(2,1)S(1)}, u32[]{:S(2)}, u32[]{:S(2)}) collective-permute-start(bf16[4,240,640]{2,1,0:T(8,128)(2,1)S(1)} %pad_maximum_fusion), channel_id=1, source_target_pairs={{0,8},{8,0},{16,24},{24,16},{32,40},{40,32},{48,56},{56,48},{64,72... | collective-permute-start | bytes 3686408 | tf_op jit(solution)/shard_map/ppermute | solution.py:559
  96.2 5.0 %copy-start = (bf16[2048,640]{1,0:T(8,128)(2,1)S(1)}, bf16[2048,640]{1,0:T(8,128)(2,1)}, u32[]{:S(2)}) copy-start(bf16[2048,640]{1,0:T(8,128)(2,1)} %q_ref.9) | copy-start | bytes 7864324
  96.3 5.0 %copy-start.1 = (f32[1,640]{1,0:T(1,128)S(1)}, f32[1,640]{1,0:T(1,128)}, u32[]{:S(2)}) copy-start(f32[1,640]{1,0:T(1,128)} %gain_ref.3) | copy-start | bytes 7684
  96.3 2.3 %collective-permute-start.11 = (bf16[4,144,640]{2,1,0:T(8,128)(2,1)S(1)}, bf16[4,144,640]{2,1,0:T(8,128)(2,1)S(1)}, u32[]{:S(2)}, u32[]{:S(2)}) collective-permute-start(bf16[4,144,640]{2,1,0:T(8,128)(2,1)S(1)} %get-tuple-element.48), channel_id=1, source_target_pairs={{0,8},{8,0},{16,24},{24,16},{32,40},{40,32},{48,56},{56,48},{64,72... | collective-permute-start | bytes 2211848 | tf_op jit(solution)/shard_map/ppermute | solution.py:559
  96.5 4.6 %collective-permute-start.12 = (bf16[4,96,640]{2,1,0:T(8,128)(2,1)S(1)}, bf16[4,96,640]{2,1,0:T(8,128)(2,1)S(1)}, u32[]{:S(2)}, u32[]{:S(2)}) collective-permute-start(bf16[4,96,640]{2,1,0:T(8,128)(2,1)S(1)} %get-tuple-element.50), channel_id=1, source_target_pairs={{0,8},{8,0},{16,24},{24,16},{32,40},{40,32},{48,56},{56,48},{64,72... | collective-permute-start | bytes 1474568 | tf_op jit(solution)/shard_map/ppermute | solution.py:559
  98.7 10.9 %collective-permute-start.15 = (bf16[144,640]{1,0:T(8,128)(2,1)S(1)}, bf16[144,640]{1,0:T(8,128)(2,1)S(1)}, u32[]{:S(2)}, u32[]{:S(2)}) collective-permute-start(bf16[144,640]{1,0:T(8,128)(2,1)S(1)} %get-tuple-element.63), channel_id=1, source_target_pairs={{0,48},{8,56},{16,0},{24,8},{32,16},{40,24},{48,32},{56,40},{64,11... | collective-permute-start | bytes 552968 | tf_op jit(solution)/shard_map/ppermute | solution.py:559
  99.9 9.6 %collective-permute-start.14 = (bf16[144,640]{1,0:T(8,128)(2,1)S(1)}, bf16[144,640]{1,0:T(8,128)(2,1)S(1)}, u32[]{:S(2)}, u32[]{:S(2)}) collective-permute-start(bf16[144,640]{1,0:T(8,128)(2,1)S(1)} %get-tuple-element.64), channel_id=1, source_target_pairs={{0,32},{8,40},{16,48},{24,56},{32,0},{40,8},{48,16},{56,24},{64,96... | collective-permute-start | bytes 552968 | tf_op jit(solution)/shard_map/ppermute | solution.py:559
  100.3 11.5 %collective-permute-start.13 = (bf16[144,640]{1,0:T(8,128)(2,1)S(1)}, bf16[144,640]{1,0:T(8,128)(2,1)S(1)}, u32[]{:S(2)}, u32[]{:S(2)}) collective-permute-start(bf16[144,640]{1,0:T(8,128)(2,1)S(1)} %get-tuple-element.65), channel_id=1, source_target_pairs={{0,16},{8,24},{16,32},{24,40},{32,48},{40,56},{48,0},{56,8},{64,80... | collective-permute-start | bytes 552968 | tf_op jit(solution)/shard_map/ppermute | solution.py:559
  111.9 11.6 %collective-permute-start.16 = (bf16[3,40,640]{2,1,0:T(8,128)(2,1)S(1)}, bf16[3,40,640]{2,1,0:T(8,128)(2,1)S(1)}, u32[]{:S(2)}, u32[]{:S(2)}) collective-permute-start(bf16[3,40,640]{2,1,0:T(8,128)(2,1)S(1)} %get-tuple-element.58), channel_id=1, source_target_pairs={{64,0},{72,8},{80,16},{88,24},{96,32},{104,40},{112,48},{120,56},{... | collective-permute-start | bytes 460808 | tf_op jit(solution)/shard_map/ppermute | solution.py:559
  113.2 6.8 %collective-permute-start.19 = (bf16[96,640]{1,0:T(8,128)(2,1)S(1)}, bf16[96,640]{1,0:T(8,128)(2,1)S(1)}, u32[]{:S(2)}, u32[]{:S(2)}) collective-permute-start(bf16[96,640]{1,0:T(8,128)(2,1)S(1)} %get-tuple-element.66), channel_id=1, source_target_pairs={{0,48},{8,56},{16,0},{24,8},{32,16},{40,24},{48,32},{56,40},{64,11... | collective-permute-start | bytes 368648 | tf_op jit(solution)/shard_map/ppermute | solution.py:559
  113.9 7.3 %collective-permute-start.18 = (bf16[96,640]{1,0:T(8,128)(2,1)S(1)}, bf16[96,640]{1,0:T(8,128)(2,1)S(1)}, u32[]{:S(2)}, u32[]{:S(2)}) collective-permute-start(bf16[96,640]{1,0:T(8,128)(2,1)S(1)} %get-tuple-element.67), channel_id=1, source_target_pairs={{0,32},{8,40},{16,48},{24,56},{32,0},{40,8},{48,16},{56,24},{64,96... | collective-permute-start | bytes 368648 | tf_op jit(solution)/shard_map/ppermute | solution.py:559
  115.5 7.3 %collective-permute-start.17 = (bf16[96,640]{1,0:T(8,128)(2,1)S(1)}, bf16[96,640]{1,0:T(8,128)(2,1)S(1)}, u32[]{:S(2)}, u32[]{:S(2)}) collective-permute-start(bf16[96,640]{1,0:T(8,128)(2,1)S(1)} %get-tuple-element.68), channel_id=1, source_target_pairs={{0,16},{8,24},{16,32},{24,40},{32,48},{40,56},{48,0},{56,8},{64,80... | collective-permute-start | bytes 368648 | tf_op jit(solution)/shard_map/ppermute | solution.py:559
where the time goes:
time: 125 us
  Pallas kernels  53.1 us (42%)
  waiting for transfers between devices  52.5 us (42%)
  starting transfers between devices  15.4 us (12%)
  local copies, waits for them, and re-layouts  2.31 us (2%)
    ppermute x20, waiting for transfers between devices, send(): return lax.ppermute(x, 'seq', pairs)  52.5 us
    pallas_call x1, Pallas kernels, gradient_second(): pl.pallas_call(body, out_shape=pieces + [jax.ShapeDtypeStruct(w.shape, BF...  17 us
    ppermute x20, starting transfers between devices, send(): return lax.ppermute(x, 'seq', pairs)  15.4 us
    pallas_call x2, Pallas kernels, attention_rest(): pl.pallas_call(body, out_shape=jax.ShapeDtypeStruct((rows, width), F32),...  13.8 us
    pallas_call x2, Pallas kernels, fast_apply(): pl.pallas_call(body, out_shape=jax.ShapeDtypeStruct((rows, width), BF16),...  12 us
    pallas_call x1, Pallas kernels, attention_first(): pl.pallas_call(body, out_shape=jax.ShapeDtypeStruct((rows, width), F32),...  4.57 us
  transfers between devices with their start and end apart: 20, of which 13 were waited for; matrix products, arithmetic and copies ran while one was open for 1% of the time, Pallas kernels for 26%

commit v1 on v0

--- a/solution.py
+++ b/solution.py
@@ -66,10 +66,13 @@
             o_ref[strip * SUB : (strip + 1) * SUB, cols] = out[:, :AH] / out[:, AH:]
 
 
-def attention_first(info, q, k, v, halo_k, halo_v, partly):
+def attention_first(info, q, k, v, halo, partly):
     rows, width = q.shape
     tile = pl.BlockSpec((WINDOW, width), lambda i, s: (0, 0))
 
+    def past(n):
+        return pl.BlockSpec((None, WINDOW, width), lambda i, s: (n, 0, 0))
+
     def body(info_ref, q_ref, kp_ref, kc_ref, vp_ref, vc_ref, _, o_ref):
         attention_body(True, info_ref, q_ref, kp_ref, kc_ref, vp_ref, vc_ref, o_ref)
 
@@ -79,13 +82,13 @@
         grid_spec=pltpu.PrefetchScalarGridSpec(
             num_scalar_prefetch=1,
             grid=(1,),
-            in_specs=[tile] * 5 + [pl.BlockSpec(memory_space=pl.ANY)],
+            in_specs=[tile, past(0), tile, past(1), tile, pl.BlockSpec(memory_space=pl.ANY)],
             out_specs=tile,
         ),
         input_output_aliases={6: 0},
         compiler_params=params(),
         name="attention_first",
-    )(info, q, halo_k, k, halo_v, v, partly)
+    )(info, q, halo, k, halo, v, partly)
 
 
 def attention_rest(info, q, k, v, block, partly=None):
@@ -139,21 +142,29 @@
 EARLY = Chunk("early", ((0, 0, 40), (1, 0, 8)))
 LATE = Chunk("late", ((1, 8, 32),))
 CHUNKS = (EARLY, LATE)
-
-
-def factors(chunk, base, w_ref, keys_ref, values_ref, rate_ref, x_ref, at):
-    n = chunk.rows
-    keys = keys_ref[at]
-    values = values_ref[at]
+UNITS = EARLY.rows + LATE.rows
+
+
+def factors(gate_pre, up_pre, back, rate_ref, x_ref, at):
     rate = rate_ref[:, at]
-    gate_pre = dot(w_ref[:n], keys, NT)
-    up_pre = dot(w_ref[n : 2 * n], keys, NT)
-    back = dot(w_ref[2 * n :], values, NT) * rate
+    back = back * rate
     sig = 0.5 * jnp.tanh(0.5 * gate_pre) + 0.5
     active = gate_pre * sig
-    x_ref[0, base : base + n, at] = (back * up_pre * (sig + active * (1.0 - sig))).astype(BF16)
-    x_ref[1, base : base + n, at] = (back * active).astype(BF16)
-    x_ref[2, base : base + n, at] = (active * up_pre * rate).astype(BF16)
+    x_ref[0, :, at] = (back * up_pre * (sig + active * (1.0 - sig))).astype(BF16)
+    x_ref[1, :, at] = (back * active).astype(BF16)
+    x_ref[2, :, at] = (active * up_pre * rate).astype(BF16)
+
+
+def tile_factors(w_ref, keys_ref, values_ref, rate_ref, x_ref, at):
+    keys = keys_ref[at]
+    factors(
+        dot(w_ref[0], keys, NT),
+        dot(w_ref[1], keys, NT),
+        dot(w_ref[2], values_ref[at], NT),
+        rate_ref,
+        x_ref,
+        at,
+    )
 
 
 TILE = 512
@@ -197,37 +208,35 @@
             base += chunk.rows
 
 
-def row_copies(chunk, info_ref, fw_hbm, rows_ref, sems):
-    half = fw_hbm.shape[1] // 2
+def order_rows(info_ref, raw_ref, w_ref, m):
+    half = raw_ref.shape[1] // 2
     owned = half // SLOTS
     z, c = info_ref[2], info_ref[3]
-    copies = []
-    for d in range(RING):
-        for e in range(2):
-            owner = 2 * lax.rem(z + d, RING) + (c if e == 0 else 1 - c)
-            at = (2 * d + e) * chunk.span
-            for h, lo, n in chunk.spans:
-                start = pl.multiple_of(owner * owned + h * half + lo, 8)
-                copies.append(
-                    pltpu.make_async_copy(
-                        fw_hbm.at[:, pl.ds(start, n)],
-                        rows_ref.at[:, pl.ds(at, n)],
-                        sems.at[len(copies)],
-                    )
-                )
-                at += n
-    return copies
-
-
-def fill_gathered(chunk, base, sources, w_ref):
-    for d in range(RING):
-        for e in range(2):
-            from_there = (-d) % RING
-            ref = sources[RING].at[from_there] if e else sources[from_there]
-            for m in range(3):
-                at = (m * SLOTS + 2 * d + e) * chunk.span
-                here = base + m * chunk.span
-                w_ref[at : at + chunk.span] = ref[here : here + chunk.span]
+    base = 0
+    for chunk in CHUNKS:
+        for d in range(RING):
+            for e in range(2):
+                owner = 2 * lax.rem(z + d, RING) + (c if e == 0 else 1 - c)
+                rows = [
+                    raw_ref[m, pl.ds(pl.multiple_of(owner * owned + h * half + lo, 8), n)]
+                    for h, lo, n in chunk.spans
+                ]
+                w_ref[m, base : base + chunk.span] = jnp.concatenate(rows, 0).astype(BF16)
+                base += chunk.span
+
+
+def fill_gathered(sources, w_ref):
+    base, at = 0, 0
+    for chunk in CHUNKS:
+        for d in range(RING):
+            for e in range(2):
+                from_there = (-d) % RING
+                ref = sources[RING].at[from_there] if e else sources[from_there]
+                for m in range(3):
+                    here = at + m * chunk.span
+                    w_ref[m, base : base + chunk.span] = ref[here : here + chunk.span]
+                base += chunk.span
+        at += 3 * chunk.span
 
 
 HERE = pl.BlockSpec(memory_space=pltpu.VMEM)
@@ -238,59 +247,68 @@
 PIECE = SPLIT + 3 * LATE.span
 
 
-def gradient_shapes(rows, width, chunked):
+def fetch(info, sources, height):
+    rows, width = sources[0].shape
+
+    def body(info_ref, *refs):
+        ins, o_ref, sems = refs[: len(sources)], refs[-2], refs[-1]
+        copies = [
+            pltpu.make_async_copy(
+                i.at[pl.ds(rows - height, height)], o_ref.at[n], sems.at[n]
+            )
+            for n, i in enumerate(ins)
+        ]
+        for copy in copies:
+            copy.start()
+        for copy in copies:
+            copy.wait()
+
+    return pl.pallas_call(
+        body,
+        out_shape=jax.ShapeDtypeStruct((len(sources), height, width), BF16),
+        grid_spec=pltpu.PrefetchScalarGridSpec(
+            num_scalar_prefetch=1,
+            grid=(1,),
+            in_specs=[ANYWHERE] * len(sources),
+            out_specs=HERE,
+            scratch_shapes=[pltpu.SemaphoreType.DMA((len(sources),))],
+        ),
+        compiler_params=params(16),
+        name="fetch",
+    )(info, *sources)
+
+
+def piece_shapes(width, chunked):
     heights = (SPLIT, PIECE - SPLIT) if chunked else (PIECE,)
-    pieces = [
+    return [
         jax.ShapeDtypeStruct((RING, height, width), BF16) for height in heights for _ in range(2)
     ]
-    scratch = [pltpu.VMEM((3 * chunk.rows, width), BF16) for chunk in CHUNKS] + [
-        pltpu.VMEM((3, sum(chunk.rows for chunk in CHUNKS), rows), BF16),
-        pltpu.VMEM((rows, width), BF16),
-        pltpu.VMEM((rows, width), BF16),
-        pltpu.SemaphoreType.DMA((2,)),
-        pltpu.SemaphoreType.DMA((2, rows // TILE)),
-    ]
-    return pieces, scratch
 
 
 def gradient_first(info, initial, keys, values, rates):
     rows, width = keys.shape
-    pieces, scratch = gradient_shapes(rows, width, False)
-    weights = [jax.ShapeDtypeStruct((3 * chunk.rows, width), BF16) for chunk in CHUNKS]
-
-    def body(info_ref, fw_hbm, key_hbm, value_hbm, rate_ref, mine, theirs, *refs):
-        outs, held, refs = refs[:2], refs[2:4], refs[4:]
-        x_ref, ks_ref, vs_ref, w_sems, t_sems, *refs = refs
-        raw, row_sems = refs[:2], refs[2:]
+
+    def body(info_ref, raw_ref, key_hbm, value_hbm, rate_ref, mine, theirs, w_out, *refs):
+        w_ref, x_ref, ks_ref, vs_ref, save_sem, t_sems = refs
 
         @pl.when(info_ref[1] == 0)
         def _():
             tokens = Tokens(key_hbm, value_hbm, ks_ref, vs_ref, t_sems)
-            fetches = [
-                row_copies(chunk, info_ref, fw_hbm, ref, sems)
-                for chunk, ref, sems in zip(CHUNKS, raw, row_sems)
-            ]
-            saves = [pltpu.make_async_copy(held[i], outs[i], w_sems.at[i]) for i in range(2)]
-
-            def part(i, t):
-                base = i * EARLY.rows
-                factors(CHUNKS[i], base, held[i], ks_ref, vs_ref, rate_ref, x_ref, tokens.at(t))
-
-            for copy in fetches[0]:
-                copy.start()
-            tokens.start(0)
-            for i, chunk in enumerate(CHUNKS):
-                for copy in fetches[i]:
-                    copy.wait()
-                if i == 0:
-                    for copy in fetches[1]:
-                        copy.start()
-                    tokens.start(1)
-                for m in range(3):
-                    held[i][m * chunk.rows : (m + 1) * chunk.rows] = raw[i][m].astype(BF16)
-                if i == 0:
-                    tokens.wait(0)
-                part(i, 0)
+            save = pltpu.make_async_copy(w_ref, w_out, save_sem)
+            first_keys, first_values = tokens.copies(0)
+            first_keys.start()
+            first_values.start()
+            tokens.start(1)
+            pre = []
+            at = pl.ds(0, TILE)
+            for m in range(3):
+                order_rows(info_ref, raw_ref, w_ref, m)
+                if m == 0:
+                    first_keys.wait()
+                if m == 2:
+                    first_values.wait()
+                pre.append(dot(w_ref[m], (vs_ref if m == 2 else ks_ref)[at], NT))
+            factors(*pre, rate_ref, x_ref, at)
 
             def one_tile(t, carry):
                 @pl.when(t + 1 < tokens.count)
@@ -298,132 +316,117 @@
                     tokens.start(t + 1)
 
                 tokens.wait(t)
-                part(0, t)
-                part(1, t)
+                tile_factors(w_ref, ks_ref, vs_ref, rate_ref, x_ref, tokens.at(t))
                 return carry
 
             lax.fori_loop(1, tokens.count, one_tile, 0)
-            for save in saves:
-                save.start()
+            save.start()
             halves = [
                 [ref.at[:, at] for ref in (mine, theirs)]
                 for at in (slice(0, SPLIT), slice(SPLIT, PIECE))
             ]
             contract(x_ref, ks_ref, vs_ref, halves)
-            for save in saves:
-                save.wait()
-
-    return pl.pallas_call(
-        body,
-        out_shape=pieces + weights,
+            save.wait()
+
+    return pl.pallas_call(
+        body,
+        out_shape=piece_shapes(width, False) + [jax.ShapeDtypeStruct((3, UNITS, width), BF16)],
         grid_spec=pltpu.PrefetchScalarGridSpec(
             num_scalar_prefetch=1,
             grid=(1,),
-            in_specs=[ANYWHERE] * 3 + [pl.BlockSpec(rates.shape, lambda i, s: (0, 0))],
-            out_specs=[HERE] * 2 + [ANYWHERE] * 2,
-            scratch_shapes=scratch
-            + [pltpu.VMEM((3, chunk.rows, width), F32) for chunk in CHUNKS]
-            + [pltpu.SemaphoreType.DMA((SLOTS * len(chunk.spans),)) for chunk in CHUNKS],
+            in_specs=[HERE] + [ANYWHERE] * 2 + [pl.BlockSpec(rates.shape, lambda i, s: (0, 0))],
+            out_specs=[HERE] * 2 + [ANYWHERE],
+            scratch_shapes=[
+                pltpu.VMEM((3, UNITS, width), BF16),
+                pltpu.VMEM((3, UNITS, rows), BF16),
+                pltpu.VMEM((rows, width), BF16),
+                pltpu.VMEM((rows, width), BF16),
+                pltpu.SemaphoreType.DMA(()),
+                pltpu.SemaphoreType.DMA((2, rows // TILE)),
+            ],
         ),
         compiler_params=params(),
         name="gradient_first",
     )(info, initial, keys, values, rates)
 
 
-def gradient_second(info, gathered, keys, values, rates, kept):
-    rows, width = keys.shape
-    pieces, scratch = gradient_shapes(rows, width, True)
+def gradient_second(info, gathered, staged, rates, kept):
+    _, rows, width = staged.shape
     count = RING + 1
 
     def body(info_ref, *refs):
         sources, refs = refs[:count], refs[count:]
-        key_hbm, value_hbm, rate_ref, _, _, ma, ta, mb, tb, *refs = refs
-        outs, held, refs = refs[:2], refs[2:4], refs[4:]
-        x_ref, ks_ref, vs_ref, w_sems, t_sems = refs
+        staged_ref, rate_ref, _, ma, ta, mb, tb, w_out, w_ref, x_ref, save_sem = refs
+        keys_ref, values_ref = staged_ref.at[0], staged_ref.at[1]
 
         @pl.when(info_ref[1] == 1)
         def _():
-            tokens = Tokens(key_hbm, value_hbm, ks_ref, vs_ref, t_sems)
-            tokens.start(0)
-            saves = [pltpu.make_async_copy(held[i], outs[i], w_sems.at[i]) for i in range(2)]
-            for i, chunk in enumerate(CHUNKS):
-                fill_gathered(chunk, i * SPLIT, sources, held[i])
+            fill_gathered(sources, w_ref)
+            save = pltpu.make_async_copy(w_ref, w_out, save_sem)
 
             def one_tile(t, carry):
-                @pl.when(t + 1 < tokens.count)
-                def _():
-                    tokens.start(t + 1)
-
-                tokens.wait(t)
-                for i, chunk in enumerate(CHUNKS):
-                    base = i * EARLY.rows
-                    factors(chunk, base, held[i], ks_ref, vs_ref, rate_ref, x_ref, tokens.at(t))
+                at = pl.ds(pl.multiple_of(t * TILE, TILE), TILE)
+                tile_factors(w_ref, keys_ref, values_ref, rate_ref, x_ref, at)
                 return carry
 
-            lax.fori_loop(0, tokens.count, one_tile, 0)
-            for save in saves:
-                save.start()
-            contract(x_ref, ks_ref, vs_ref, ((ma, ta), (mb, tb)))
-            for save in saves:
-                save.wait()
-
-    return pl.pallas_call(
-        body,
-        out_shape=pieces + [jax.ShapeDtypeStruct(w.shape, BF16) for w in kept],
+            lax.fori_loop(0, rows // TILE, one_tile, 0)
+            save.start()
+            contract(x_ref, keys_ref, values_ref, ((ma, ta), (mb, tb)))
+            save.wait()
+
+    return pl.pallas_call(
+        body,
+        out_shape=piece_shapes(width, True) + [jax.ShapeDtypeStruct(kept.shape, BF16)],
         grid_spec=pltpu.PrefetchScalarGridSpec(
             num_scalar_prefetch=1,
             grid=(1,),
-            in_specs=[HERE] * count
-            + [ANYWHERE] * 2
-            + [pl.BlockSpec(rates.shape, lambda i, s: (0, 0))]
-            + [ANYWHERE] * 2,
-            out_specs=[HERE] * 4 + [ANYWHERE] * 2,
-            scratch_shapes=scratch,
-        ),
-        input_output_aliases={count + 4: 4, count + 5: 5},
-        compiler_params=params(),
+            in_specs=[HERE] * (count + 1)
+            + [pl.BlockSpec(rates.shape, lambda i, s: (0, 0)), ANYWHERE],
+            out_specs=[HERE] * 4 + [ANYWHERE],
+            scratch_shapes=[
+                pltpu.VMEM((3, UNITS, width), BF16),
+                pltpu.VMEM((3, UNITS, rows), BF16),
+                pltpu.SemaphoreType.DMA(()),
+            ],
+        ),
+        input_output_aliases={count + 3: 4},
+        compiler_params=params(30),
         name="gradient_second",
-    )(info, *gathered, keys, values, rates, *kept)
-
-
-def partial_output(q, w_ref):
-    n = w_ref.shape[0] // 3
-    gate_pre = dot(q, w_ref[:n], NT)
-    up_pre = dot(q, w_ref[n : 2 * n], NT)
-    sig = 0.5 * jnp.tanh(0.5 * gate_pre) + 0.5
-    return dot((gate_pre * sig * up_pre).astype(BF16), w_ref[2 * n :], NN)
-
-
-def fast_apply(info, queries, weights, gain, attended, tiles, partly=None, tile=512):
+    )(info, *gathered, staged, rates, kept)
+
+
+def fast_apply(info, queries, weights, gain, attended, tile=512):
     rows, width = queries.shape
-    stream = pl.BlockSpec((tile, width), lambda i, s: (i + tiles[0], 0))
-    kept = [] if partly is None else [partly]
-
-    def body(info_ref, q_ref, early_ref, late_ref, gain_ref, att_ref, *rest):
+    stream = pl.BlockSpec((tile, width), lambda i, s: (i, 0))
+
+    def body(info_ref, q_ref, w_ref, gain_ref, att_ref, o_ref):
         q = q_ref[...]
-        out = partial_output(q, early_ref) + partial_output(q, late_ref)
+        gate_pre = dot(q, w_ref[0], NT)
+        up_pre = dot(q, w_ref[1], NT)
+        sig = 0.5 * jnp.tanh(0.5 * gate_pre) + 0.5
+        out = dot((gate_pre * sig * up_pre).astype(BF16), w_ref[2], NN)
         inverse_rms = lax.rsqrt(jnp.mean(out * out, axis=-1, keepdims=True) + EPSILON)
-        rest[-1][...] = (att_ref[...] + out * inverse_rms * gain_ref[...]).astype(BF16)
+        o_ref[...] = (att_ref[...] + out * inverse_rms * gain_ref[...]).astype(BF16)
 
     return pl.pallas_call(
         body,
         out_shape=jax.ShapeDtypeStruct((rows, width), BF16),
         grid_spec=pltpu.PrefetchScalarGridSpec(
             num_scalar_prefetch=1,
-            grid=(tiles[1] - tiles[0],),
-            in_specs=[stream]
-            + [
-                pl.BlockSpec(w.shape, lambda i, s: (0, 0), pipeline_mode=pl.Buffered(1))
-                for w in weights
-            ]
-            + [pl.BlockSpec((1, width), lambda i, s: (0, 0)), stream]
-            + [ANYWHERE for _ in kept],
+            grid=(rows // tile,),
+            in_specs=[
+                stream,
+                pl.BlockSpec(
+                    weights.shape, lambda i, s: (0, 0, 0), pipeline_mode=pl.Buffered(1)
+                ),
+                pl.BlockSpec((1, width), lambda i, s: (0, 0)),
+                stream,
+            ],
             out_specs=stream,
         ),
-        input_output_aliases={6: 0} if kept else {},
         compiler_params=params(32),
-        name=f"fast_apply_{tiles[0]}",
-    )(info, queries, *weights, gain, attended, *kept)
+        name="fast_apply",
+    )(info, queries, weights, gain, attended)
 
 
 def renormalize(previous, gradient):
@@ -479,8 +482,8 @@
     )(info, mine, other, *arrived, fast_weights, fast_weights)
 
 
-def sum_body(mine_ref, other_ref, a_ref, b_ref, c_ref, near_ref, far_ref):
-    gradient = total(mine_ref, other_ref, a_ref, b_ref, c_ref)
+def sum_body(mine_ref, other_ref, a_ref, b_ref, both_ref, near_ref, far_ref):
+    gradient = total(mine_ref, other_ref, a_ref, b_ref, both_ref.at[:SPLIT])
     owned, rest = near_ref.shape[1], far_ref.shape[1]
     for m in range(3):
         at = m * (owned + rest)
@@ -507,13 +510,13 @@
 def final_far(info, mine, other, arrived, cast, far):
     shape = (3, EARLY.spans[0][2], cast.shape[1])
 
-    def body(info_ref, mine_ref, other_ref, a_ref, b_ref, c_ref, cast_ref, far_ref, o_ref):
+    def body(info_ref, mine_ref, other_ref, a_ref, b_ref, both_ref, cast_ref, far_ref, o_ref):
         rest = far_ref.shape[1]
         owned = EARLY.span - rest
 
         @pl.when(info_ref[1] == 1)
         def _():
-            gradient = total(mine_ref, other_ref, a_ref, b_ref, c_ref)
+            gradient = total(mine_ref, other_ref, a_ref, b_ref, both_ref.at[SPLIT:])
             for m in range(3):
                 at = m * EARLY.span
                 early = cast_ref[at : at + EARLY.span].astype(F32)[owned:]
@@ -528,6 +531,9 @@
         grid_spec=pltpu.PrefetchScalarGridSpec(
             num_scalar_prefetch=1, grid=(1,), in_specs=[HERE] * 7, out_specs=HERE
         ),
+        cost_estimate=pl.CostEstimate(
+            flops=40_000_000_000, bytes_accessed=100_000_000, transcendentals=0
+        ),
         compiler_params=params(16),
         name="final_far",
     )(info, mine, other, *arrived, cast, far)
@@ -597,43 +603,44 @@
     row_count, width = attn_query.shape
     seq = lax.axis_index("seq").astype(jnp.int32)
     info = jnp.stack([seq, seq // 8, (seq % 8) // 2, seq % 2])
-    initial = in_hbm(jnp.transpose(fast_weights[0], (1, 0, 2)))
+    initial = jnp.transpose(fast_weights[0], (1, 0, 2))
     tokens = (in_hbm(fast_key), in_hbm(fast_value), in_hbm(rates.reshape(1, row_count)))
     attn = tuple(in_hbm(x) for x in (attn_query, attn_key, attn_value))
 
     onward = [(i, (i + 1) % 16) for i in range(16)]
-    tails = [x[row_count - WINDOW :] for x in (attn_key, attn_value)]
-
-    mine, theirs, *weights = gradient_first(after(info, *tails), initial, *tokens)
-    halo = [send(tail, onward) for tail in tails]
-    other = send(after(theirs, *halo), SIBLING)
-    parts = joined(mine, other)
+    tails = fetch(info, attn[1:], WINDOW)
+
+    mine, theirs, weights = gradient_first(after(info, tails), initial, *tokens)
+    halo = send(tails, onward)
+    other = send(theirs, SIBLING)
+    parts = joined(after(mine, halo), other)
     ring = around(parts)
     attended = attention_rest(after(info, *parts), *attn, 1)
     cast, middle = middle_call(after(info, attended), mine, other, ring, initial)
     own = send(cast, ACROSS)
     attended = attention_rest(after(info, cast), *attn, 0, attended)
 
-    own = after(own, attended)
+    staged = fetch(after(info, attended), tokens[:2], row_count)
+    own = after(own, staged)
     ring = around([own] * (RING - 1))
-    attended = attention_first(after(info, own), *attn, *halo, attended)
+    attended = attention_first(after(info, own, staged), *attn, halo, attended)
     column = [own] + [after(piece, attended) for piece in ring]
     beside = send(jnp.stack(column), SIBLING)
-    mine_a, theirs_a, mine_b, theirs_b, *weights = gradient_second(
-        info, [*column, beside], *tokens, weights
+    mine_a, theirs_a, mine_b, theirs_b, weights = gradient_second(
+        info, [*column, beside], staged, tokens[2], weights
     )
     other_a = send(theirs_a, SIBLING)
     other_b = send(theirs_b, SIBLING)
     part_a = joined(mine_a, other_a)
-    ring_a = around(part_a)
-    part_b = joined(after(mine_b, *part_a), other_b)
-    apply = partial(fast_apply, queries=fast_query, weights=weights, gain=gain, attended=attended)
-    mixed = apply(after(info, *part_b), tiles=(0, 3))
-    near, far = sum_call(after(mine_a, mixed), other_a, ring_a)
+    part_b = joined(mine_b, other_b)
+    both = jnp.concatenate([part_a[1], part_b[1]], 0)
+    ring_a = [send(part_a[0], along_z(1)), send(part_a[2], along_z(3))]
+    ring_b = [send(part_b[0], along_z(1)), send(part_b[2], along_z(3))]
+    both = send(both, along_z(2))
+    mixed = fast_apply(after(info, *part_a, *part_b), fast_query, weights, gain, attended)
+    near, far = sum_call(after(mine_a, mixed), other_a, [*ring_a, both])
     near = send(near, BACK)
-    ring_b = around(part_b)
-    mixed = apply(after(info, far), tiles=(3, 4), partly=mixed)
-    far_rows = final_far(after(info, mixed), mine_b, other_b, ring_b, own, far)
+    far_rows = final_far(after(info, far), mine_b, other_b, [*ring_b, both], own, far)
     final = final_near(info, middle, near, far_rows)
     return mixed, jnp.transpose(final, (1, 0, 2))[None]
 

time: 125 us -> 120 us (0.960)
  the two profiles are of different devices: /device:TPU:30 before, /device:TPU:0 now
where the time goes in v1:
time: 120 us
  Pallas kernels  54.6 us (46%)
  waiting for transfers between devices  45.4 us (38%)
  starting transfers between devices  17.5 us (15%)
    ppermute x18, waiting for transfers between devices, send(): return lax.ppermute(x, 'seq', pairs)  45.4 us
    ppermute x18, starting transfers between devices, send(): return lax.ppermute(x, 'seq', pairs)  17.5 us
    pallas_call x1, Pallas kernels, gradient_first(): pl.pallas_call(body, out_shape=piece_shapes(width, False) + [jax.ShapeDty...  17.1 us
    pallas_call x2, Pallas kernels, attention_rest(): pl.pallas_call(body, out_shape=jax.ShapeDtypeStruct((rows, width), F32),...  13.2 us
    pallas_call x1, Pallas kernels, fast_apply(): pl.pallas_call(body, out_shape=jax.ShapeDtypeStruct((rows, width), BF16),...  10.3 us
    pallas_call x2, Pallas kernels, fetch(): pl.pallas_call(body, out_shape=jax.ShapeDtypeStruct((len(sources), height...  5.2 us
    pallas_call x1, Pallas kernels, attention_first(): pl.pallas_call(body, out_shape=jax.ShapeDtypeStruct((rows, width), F32),...  4.61 us
  transfers between devices with their start and end apart: 18, of which 11 were waited for; matrix products, arithmetic and copies ran while one was open for 0% of the time, Pallas kernels for 41%

profile of v1, /device:TPU:0, one launch (start us, length us, event | category | flops | bytes accessed | tf_op | source)
XLA Modules:
  0.0 119.7 jit_solution(9788309162722916066)
XLA Ops:
  0.8 2.1 %fetch.2 = bf16[2,512,640]{2,1,0:T(8,128)(2,1)S(1)} custom-call(s32[4]{0:T(128)S(1)} %pad_add_fusion.info_ref, bf16[2048,640]{1,0:T(8,128)(2,1)} %kc_ref.5, bf16[2048,640]{1,0:T(8,128)(2,1)} %vc_ref.5), custom_call_target="tpu_custom_call" | custom-call | tf_op jit(solution)/shard_map/fetch/pallas_call | solution.py:266
  3.5 17.1 %gradient_first.1 = (bf16[4,240,640]{2,1,0:T(8,128)(2,1)S(1)}, bf16[4,240,640]{2,1,0:T(8,128)(2,1)S(1)}, bf16[3,640,640]{2,1,0:T(8,128)(2,1)S(1)}) custom-call(s32[4]{0:T(128)S(1)} %pad_add_fusion.info_ref, f32[3,640,640]{2,1,0:T(8,128)S(1)} %bitcast.33, bf16[2048,640]{1,0:T(8,128)(2,1)} %refs_0_.3, bf16[2048,640]{1,0:T(8,128)(2,1)} %refs_1_.3, ...), custom_call_target="tpu_custom_call" | custom-call | tf_op jit(solution)/shard_map/gradient_first/pallas_call | solution.py:331
  20.6 1.6 %collective-permute-start.1 = (bf16[4,240,640]{2,1,0:T(8,128)(2,1)S(1)}, bf16[4,240,640]{2,1,0:T(8,128)(2,1)S(1)}, u32[]{:S(2)}, u32[]{:S(2)}) collective-permute-start(bf16[4,240,640]{2,1,0:T(8,128)(2,1)S(1)} %get-tuple-element.31), channel_id=1, source_target_pairs={{0,8},{8,0},{16,24},{24,16},{32,40},{40,32},{48,56},{56,48},{64,72... | collective-permute-start | bytes 3686408 | tf_op jit(solution)/shard_map/ppermute | solution.py:565
  22.2 2.2 %collective-permute-done.kp_ref.vp_ref = bf16[2,512,640]{2,1,0:T(8,128)(2,1)S(1)} collective-permute-done((bf16[2,512,640]{2,1,0:T(8,128)(2,1)S(1)}, bf16[2,512,640]{2,1,0:T(8,128)(2,1)S(1)}, u32[]{:S(2)}, u32[]{:S(2)}) %collective-permute-start) | collective-permute-done | bytes 1310752 | tf_op jit(solution)/shard_map/ppermute | solution.py:565
  25.0 4.0 %collective-permute-start.4 = (bf16[240,640]{1,0:T(8,128)(2,1)S(1)}, bf16[240,640]{1,0:T(8,128)(2,1)S(1)}, u32[]{:S(2)}, u32[]{:S(2)}) collective-permute-start(bf16[240,640]{1,0:T(8,128)(2,1)S(1)} %get-tuple-element.54), channel_id=1, source_target_pairs={{0,48},{8,56},{16,0},{24,8},{32,16},{40,24},{48,32},{56,40},{64,11... | collective-permute-start | bytes 921608 | tf_op jit(solution)/shard_map/ppermute | solution.py:565
  30.1 2.4 %attention_rest_1.1.rest_0_ = f32[2048,640]{1,0:T(8,128)S(1)} custom-call(s32[4]{0:T(128)S(1)} %pad_add_fusion.info_ref, bf16[2048,640]{1,0:T(8,128)(2,1)} %q_ref.6, bf16[2048,640]{1,0:T(8,128)(2,1)} %kc_ref.5, bf16[2048,640]{1,0:T(8,128)(2,1)} %kc_ref.5, bf16[2048,640]{1,0:T(8,128)(2,1)} %vc_ref.5, bf16[2048,640]{1,0:T(8,128)(2,1)} %vc_ref.5), custom_call_target="tpu_custom_call" | custom-call | tf_op jit(solution)/shard_map/attention_rest_1/pallas_call | solution.py:114
  32.5 10.1 %collective-permute-done.4.c_ref = bf16[240,640]{1,0:T(8,128)(2,1)S(1)} collective-permute-done((bf16[240,640]{1,0:T(8,128)(2,1)S(1)}, bf16[240,640]{1,0:T(8,128)(2,1)S(1)}, u32[]{:S(2)}, u32[]{:S(2)}) %collective-permute-start.4) | collective-permute-done | bytes 307232 | tf_op jit(solution)/shard_map/ppermute | solution.py:565
  42.7 3.4 %collective-permute-done.2.a_ref = bf16[240,640]{1,0:T(8,128)(2,1)S(1)} collective-permute-done((bf16[240,640]{1,0:T(8,128)(2,1)S(1)}, bf16[240,640]{1,0:T(8,128)(2,1)S(1)}, u32[]{:S(2)}, u32[]{:S(2)}) %collective-permute-start.2) | collective-permute-done | bytes 307232 | tf_op jit(solution)/shard_map/ppermute | solution.py:565
  47.0 1.3 %collective-permute-start.5 = (bf16[240,640]{1,0:T(8,128)(2,1)S(1)}, bf16[240,640]{1,0:T(8,128)(2,1)S(1)}, u32[]{:S(2)}, u32[]{:S(2)}) collective-permute-start(bf16[240,640]{1,0:T(8,128)(2,1)S(1)} %get-tuple-element.34), channel_id=1, source_target_pairs={{0,64},{8,72},{16,80},{24,88},{32,96},{40,104},{48,112},{56,120},{... | collective-permute-start | bytes 921608 | tf_op jit(solution)/shard_map/ppermute | solution.py:565
  48.3 10.7 %attention_rest_0.1._ = f32[2048,640]{1,0:T(8,128)S(1)} custom-call(s32[4]{0:T(128)S(1)} %pad_add_fusion.info_ref, bf16[2048,640]{1,0:T(8,128)(2,1)} %q_ref.6, bf16[2048,640]{1,0:T(8,128)(2,1)} %kc_ref.5, bf16[2048,640]{1,0:T(8,128)(2,1)} %kc_ref.5, bf16[2048,640]{1,0:T(8,128)(2,1)} %vc_ref.5, ...), custom_call_target="tpu_custom_call", output_to_operand_aliasing={{}: (6, {})} | custom-call | tf_op jit(solution)/shard_map/attention_rest_0/pallas_call | solution.py:114
  59.1 3.1 %fetch.3.refs_5_ = bf16[2,2048,640]{2,1,0:T(8,128)(2,1)S(1)} custom-call(s32[4]{0:T(128)S(1)} %pad_add_fusion.info_ref, bf16[2048,640]{1,0:T(8,128)(2,1)} %refs_0_.3, bf16[2048,640]{1,0:T(8,128)(2,1)} %refs_1_.3), custom_call_target="tpu_custom_call" | custom-call | tf_op jit(solution)/shard_map/fetch/pallas_call | solution.py:266
  64.3 4.6 %attention_first.1.att_ref = f32[2048,640]{1,0:T(8,128)S(1)} custom-call(s32[4]{0:T(128)S(1)} %pad_add_fusion.info_ref, bf16[2048,640]{1,0:T(8,128)(2,1)} %q_ref.6, bf16[2,512,640]{2,1,0:T(8,128)(2,1)S(1)} %collective-permute-done.kp_ref.vp_ref, bf16[2048,640]{1,0:T(8,128)(2,1)} %kc_ref.5, ...), custom_call_target="tpu_custom_call", output_to_operand_aliasing={{}: (6, {})} | custom-call | tf_op jit(solution)/shard_map/attention_first/pallas_call | solution.py:79
  68.9 3.5 %collective-permute-done.8.refs_3_ = bf16[240,640]{1,0:T(8,128)(2,1)S(1)} collective-permute-done((bf16[240,640]{1,0:T(8,128)(2,1)S(1)}, bf16[240,640]{1,0:T(8,128)(2,1)S(1)}, u32[]{:S(2)}, u32[]{:S(2)}) %collective-permute-start.8) | collective-permute-done | bytes 307232 | tf_op jit(solution)/shard_map/ppermute | solution.py:565
  72.4 2.5 %collective-permute-done.7.refs_2_ = bf16[240,640]{1,0:T(8,128)(2,1)S(1)} collective-permute-done((bf16[240,640]{1,0:T(8,128)(2,1)S(1)}, bf16[240,640]{1,0:T(8,128)(2,1)S(1)}, u32[]{:S(2)}, u32[]{:S(2)}) %collective-permute-start.7) | collective-permute-done | bytes 307232 | tf_op jit(solution)/shard_map/ppermute | solution.py:565
  74.9 4.5 %collective-permute-done.6.refs_1_ = bf16[240,640]{1,0:T(8,128)(2,1)S(1)} collective-permute-done((bf16[240,640]{1,0:T(8,128)(2,1)S(1)}, bf16[240,640]{1,0:T(8,128)(2,1)S(1)}, u32[]{:S(2)}, u32[]{:S(2)}) %collective-permute-start.6) | collective-permute-done | bytes 307232 | tf_op jit(solution)/shard_map/ppermute | solution.py:565
  79.7 2.9 %collective-permute-done.9.refs_4_ = bf16[4,240,640]{2,1,0:T(8,128)(2,1)S(1)} collective-permute-done((bf16[4,240,640]{2,1,0:T(8,128)(2,1)S(1)}, bf16[4,240,640]{2,1,0:T(8,128)(2,1)S(1)}, u32[]{:S(2)}, u32[]{:S(2)}) %collective-permute-start.9) | collective-permute-done | bytes 1228832 | tf_op jit(solution)/shard_map/ppermute | solution.py:565
  82.6 1.2 %gradient_second.1 = (bf16[4,144,640]{2,1,0:T(8,128)(2,1)S(1)}, bf16[4,144,640]{2,1,0:T(8,128)(2,1)S(1)}, bf16[4,96,640]{2,1,0:T(8,128)(2,1)S(1)}, bf16[4,96,640...) custom-call(s32[4]{0:T(128)S(1)} %pad_add_fusion.info_ref, ...), custom_call_target="tpu_custom_call", output_to_operand_aliasing={{4}: (8, {})} | custom-call | tf_op jit(solution)/shard_map/gradient_second/pallas_call | solution.py:377
  84.4 2.4 %collective-permute-done.11.other_ref = bf16[4,96,640]{2,1,0:T(8,128)(2,1)S(1)} collective-permute-done((bf16[4,96,640]{2,1,0:T(8,128)(2,1)S(1)}, bf16[4,96,640]{2,1,0:T(8,128)(2,1)S(1)}, u32[]{:S(2)}, u32[]{:S(2)}) %collective-permute-start.11) | collective-permute-done | bytes 491552 | tf_op jit(solution)/shard_map/ppermute | solution.py:565
  88.0 1.2 %collective-permute-start.13 = (bf16[144,640]{1,0:T(8,128)(2,1)S(1)}, bf16[144,640]{1,0:T(8,128)(2,1)S(1)}, u32[]{:S(2)}, u32[]{:S(2)}) collective-permute-start(bf16[144,640]{1,0:T(8,128)(2,1)S(1)} %get-tuple-element.57), channel_id=1, source_target_pairs={{0,48},{8,56},{16,0},{24,8},{32,16},{40,24},{48,32},{56,40},{64,11... | collective-permute-start | bytes 552968 | tf_op jit(solution)/shard_map/ppermute | solution.py:565
  90.0 2.4 %collective-permute-start.17 = (bf16[96,640]{1,0:T(8,128)(2,1)S(1)}, bf16[96,640]{1,0:T(8,128)(2,1)S(1)}, u32[]{:S(2)}, u32[]{:S(2)}) collective-permute-start(bf16[96,640]{1,0:T(8,128)(2,1)S(1)} %get-tuple-element.60), channel_id=1, source_target_pairs={{0,48},{8,56},{16,0},{24,8},{32,16},{40,24},{48,32},{56,40},{64,11... | collective-permute-start | bytes 368648 | tf_op jit(solution)/shard_map/ppermute | solution.py:565
  92.5 10.3 %fast_apply.1 = bf16[2048,640]{1,0:T(8,128)(2,1)} custom-call(s32[4]{0:T(128)S(1)} %pad_add_fusion.info_ref, bf16[2048,640]{1,0:T(8,128)(2,1)S(1)} %copy-done.1, bf16[3,640,640]{2,1,0:T(8,128)(2,1)S(1)} %get-tuple-element.48.w_ref, f32[1,640]{1,0:T(1,128)S(1)} %copy-done.2, f32[2048,640]{1,0:T(8,128)S(1)} %attention_first.1.att_ref), custom_call_target="tpu_custom_call" | custom-call | tf_op jit(solution)/shard_map/fast_apply/pallas_call | solution.py:411
  102.9 1.3 %collective-permute-start.15 = (bf16[3,40,640]{2,1,0:T(8,128)(2,1)S(1)}, bf16[3,40,640]{2,1,0:T(8,128)(2,1)S(1)}, u32[]{:S(2)}, u32[]{:S(2)}) collective-permute-start(bf16[3,40,640]{2,1,0:T(8,128)(2,1)S(1)} %get-tuple-element.51), channel_id=1, source_target_pairs={{64,0},{72,8},{80,16},{88,24},{96,32},{104,40},{112,48},{120,56},{... | collective-permute-start | bytes 460808 | tf_op jit(solution)/shard_map/ppermute | solution.py:565
  105.1 13.2 %collective-permute-done.15.near_ref = bf16[3,40,640]{2,1,0:T(8,128)(2,1)S(1)} collective-permute-done((bf16[3,40,640]{2,1,0:T(8,128)(2,1)S(1)}, bf16[3,40,640]{2,1,0:T(8,128)(2,1)S(1)}, u32[]{:S(2)}, u32[]{:S(2)}) %collective-permute-start.15) | collective-permute-done | bytes 153632 | tf_op jit(solution)/shard_map/ppermute | solution.py:565
  118.3 1.4 %final_near.1 = f32[3,40,640]{2,1,0:T(8,128)} custom-call(s32[4]{0:T(128)S(1)} %pad_add_fusion.info_ref, f32[3,40,640]{2,1,0:T(8,128)S(1)} %get-tuple-element.49.middle_ref, bf16[3,40,640]{2,1,0:T(8,128)(2,1)S(1)} %collective-permute-done.15.near_ref, f32[3,40,640]{2,1,0:T(8,128)S(1)} %final_far.1.far_ref), custom_call_target="tpu_custom_call" | custom-call | tf_op jit(solution)/shard_map/final_near/pallas_call | solution.py:553
  (36 shorter events, 9.3 us)
Async XLA Ops:
  0.8 2.8 %copy-start = (f32[1,640,3,640]{3,1,2,0:T(8,128)S(1)}, f32[1,640,3,640]{3,1,2,0:T(8,128)}, u32[]{:S(2)}) copy-start(f32[1,640,3,640]{3,1,2,0:T(8,128)} %param.16) | copy-start | bytes 14745604
  2.9 21.6 %collective-permute-start = (bf16[2,512,640]{2,1,0:T(8,128)(2,1)S(1)}, bf16[2,512,640]{2,1,0:T(8,128)(2,1)S(1)}, u32[]{:S(2)}, u32[]{:S(2)}) collective-permute-start(bf16[2,512,640]{2,1,0:T(8,128)(2,1)S(1)} %fetch.2), channel_id=1, source_target_pairs={{0,8},{8,16},{16,24},{24,32},{32,40},{40,48},{48,56},{56,64},{64,7... | collective-permute-start | bytes 3932168 | tf_op jit(solution)/shard_map/ppermute | solution.py:565
  20.6 4.1 %collective-permute-start.1 = (bf16[4,240,640]{2,1,0:T(8,128)(2,1)S(1)}, bf16[4,240,640]{2,1,0:T(8,128)(2,1)S(1)}, u32[]{:S(2)}, u32[]{:S(2)}) collective-permute-start(bf16[4,240,640]{2,1,0:T(8,128)(2,1)S(1)} %get-tuple-element.31), channel_id=1, source_target_pairs={{0,8},{8,0},{16,24},{24,16},{32,40},{40,32},{48,56},{56,48},{64,72... | collective-permute-start | bytes 3686408 | tf_op jit(solution)/shard_map/ppermute | solution.py:565
  25.0 17.7 %collective-permute-start.4 = (bf16[240,640]{1,0:T(8,128)(2,1)S(1)}, bf16[240,640]{1,0:T(8,128)(2,1)S(1)}, u32[]{:S(2)}, u32[]{:S(2)}) collective-permute-start(bf16[240,640]{1,0:T(8,128)(2,1)S(1)} %get-tuple-element.54), channel_id=1, source_target_pairs={{0,48},{8,56},{16,0},{24,8},{32,16},{40,24},{48,32},{56,40},{64,11... | collective-permute-start | bytes 921608 | tf_op jit(solution)/shard_map/ppermute | solution.py:565
  29.0 13.6 %collective-permute-start.3 = (bf16[240,640]{1,0:T(8,128)(2,1)S(1)}, bf16[240,640]{1,0:T(8,128)(2,1)S(1)}, u32[]{:S(2)}, u32[]{:S(2)}) collective-permute-start(bf16[240,640]{1,0:T(8,128)(2,1)S(1)} %get-tuple-element.55), channel_id=1, source_target_pairs={{0,32},{8,40},{16,48},{24,56},{32,0},{40,8},{48,16},{56,24},{64,96... | collective-permute-start | bytes 921608 | tf_op jit(solution)/shard_map/ppermute | solution.py:565
  29.1 17.0 %collective-permute-start.2 = (bf16[240,640]{1,0:T(8,128)(2,1)S(1)}, bf16[240,640]{1,0:T(8,128)(2,1)S(1)}, u32[]{:S(2)}, u32[]{:S(2)}) collective-permute-start(bf16[240,640]{1,0:T(8,128)(2,1)S(1)} %get-tuple-element.56), channel_id=1, source_target_pairs={{0,16},{8,24},{16,32},{24,40},{32,48},{40,56},{48,0},{56,8},{64,80... | collective-permute-start | bytes 921608 | tf_op jit(solution)/shard_map/ppermute | solution.py:565
  47.0 15.1 %collective-permute-start.5 = (bf16[240,640]{1,0:T(8,128)(2,1)S(1)}, bf16[240,640]{1,0:T(8,128)(2,1)S(1)}, u32[]{:S(2)}, u32[]{:S(2)}) collective-permute-start(bf16[240,640]{1,0:T(8,128)(2,1)S(1)} %get-tuple-element.34), channel_id=1, source_target_pairs={{0,64},{8,72},{16,80},{24,88},{32,96},{40,104},{48,112},{56,120},{... | collective-permute-start | bytes 921608 | tf_op jit(solution)/shard_map/ppermute | solution.py:565
  62.2 10.2 %collective-permute-start.8 = (bf16[240,640]{1,0:T(8,128)(2,1)S(1)}, bf16[240,640]{1,0:T(8,128)(2,1)S(1)}, u32[]{:S(2)}, u32[]{:S(2)}) collective-permute-start(bf16[240,640]{1,0:T(8,128)(2,1)S(1)} %collective-permute-done.5.refs_0_.cast_ref), channel_id=1, source_target_pairs={{0,48},{8,56},{16,0},{24,8},{32,16},{40,24},{48,32},{56,40},{64,11... | collective-permute-start | bytes 921608 | tf_op jit(solution)/shard_map/ppermute | solution.py:565
  63.1 11.8 %collective-permute-start.7 = (bf16[240,640]{1,0:T(8,128)(2,1)S(1)}, bf16[240,640]{1,0:T(8,128)(2,1)S(1)}, u32[]{:S(2)}, u32[]{:S(2)}) collective-permute-start(bf16[240,640]{1,0:T(8,128)(2,1)S(1)} %collective-permute-done.5.refs_0_.cast_ref), channel_id=1, source_target_pairs={{0,32},{8,40},{16,48},{24,56},{32,0},{40,8},{48,16},{56,24},{64,96... | collective-permute-start | bytes 921608 | tf_op jit(solution)/shard_map/ppermute | solution.py:565
  63.4 15.9 %collective-permute-start.6 = (bf16[240,640]{1,0:T(8,128)(2,1)S(1)}, bf16[240,640]{1,0:T(8,128)(2,1)S(1)}, u32[]{:S(2)}, u32[]{:S(2)}) collective-permute-start(bf16[240,640]{1,0:T(8,128)(2,1)S(1)} %collective-permute-done.5.refs_0_.cast_ref), channel_id=1, source_target_pairs={{0,16},{8,24},{16,32},{24,40},{32,48},{40,56},{48,0},{56,8},{64,80... | collective-permute-start | bytes 921608 | tf_op jit(solution)/shard_map/ppermute | solution.py:565
  79.6 3.0 %collective-permute-start.9 = (bf16[4,240,640]{2,1,0:T(8,128)(2,1)S(1)}, bf16[4,240,640]{2,1,0:T(8,128)(2,1)S(1)}, u32[]{:S(2)}, u32[]{:S(2)}) collective-permute-start(bf16[4,240,640]{2,1,0:T(8,128)(2,1)S(1)} %pad_maximum_fusion), channel_id=1, source_target_pairs={{0,8},{8,0},{16,24},{24,16},{32,40},{40,32},{48,56},{56,48},{64,72... | collective-permute-start | bytes 3686408 | tf_op jit(solution)/shard_map/ppermute | solution.py:565
  83.8 3.1 %collective-permute-start.10 = (bf16[4,144,640]{2,1,0:T(8,128)(2,1)S(1)}, bf16[4,144,640]{2,1,0:T(8,128)(2,1)S(1)}, u32[]{:S(2)}, u32[]{:S(2)}) collective-permute-start(bf16[4,144,640]{2,1,0:T(8,128)(2,1)S(1)} %get-tuple-element.44), channel_id=1, source_target_pairs={{0,8},{8,0},{16,24},{24,16},{32,40},{40,32},{48,56},{56,48},{64,72... | collective-permute-start | bytes 2211848 | tf_op jit(solution)/shard_map/ppermute | solution.py:565
  84.0 2.8 %collective-permute-start.11 = (bf16[4,96,640]{2,1,0:T(8,128)(2,1)S(1)}, bf16[4,96,640]{2,1,0:T(8,128)(2,1)S(1)}, u32[]{:S(2)}, u32[]{:S(2)}) collective-permute-start(bf16[4,96,640]{2,1,0:T(8,128)(2,1)S(1)} %get-tuple-element.46), channel_id=1, source_target_pairs={{0,8},{8,0},{16,24},{24,16},{32,40},{40,32},{48,56},{56,48},{64,72... | collective-permute-start | bytes 1474568 | tf_op jit(solution)/shard_map/ppermute | solution.py:565
  86.8 5.7 %copy-start.1 = (bf16[2048,640]{1,0:T(8,128)(2,1)S(1)}, bf16[2048,640]{1,0:T(8,128)(2,1)}, u32[]{:S(2)}) copy-start(bf16[2048,640]{1,0:T(8,128)(2,1)} %q_ref.7) | copy-start | bytes 7864324
  86.9 5.6 %copy-start.2 = (f32[1,640]{1,0:T(1,128)S(1)}, f32[1,640]{1,0:T(1,128)}, u32[]{:S(2)}) copy-start(f32[1,640]{1,0:T(1,128)} %gain_ref.1) | copy-start | bytes 7684
  87.1 15.7 %collective-permute-start.14 = (bf16[240,640]{1,0:T(8,128)(2,1)S(1)}, bf16[240,640]{1,0:T(8,128)(2,1)S(1)}, u32[]{:S(2)}, u32[]{:S(2)}) collective-permute-start(bf16[240,640]{1,0:T(8,128)(2,1)S(1)} %pad_maximum_fusion.1), channel_id=1, source_target_pairs={{0,32},{8,40},{16,48},{24,56},{32,0},{40,8},{48,16},{56,24},{64,96... | collective-permute-start | bytes 921608 | tf_op jit(solution)/shard_map/ppermute | solution.py:565
  88.0 14.8 %collective-permute-start.13 = (bf16[144,640]{1,0:T(8,128)(2,1)S(1)}, bf16[144,640]{1,0:T(8,128)(2,1)S(1)}, u32[]{:S(2)}, u32[]{:S(2)}) collective-permute-start(bf16[144,640]{1,0:T(8,128)(2,1)S(1)} %get-tuple-element.57), channel_id=1, source_target_pairs={{0,48},{8,56},{16,0},{24,8},{32,16},{40,24},{48,32},{56,40},{64,11... | collective-permute-start | bytes 552968 | tf_op jit(solution)/shard_map/ppermute | solution.py:565
  89.2 13.6 %collective-permute-start.12 = (bf16[144,640]{1,0:T(8,128)(2,1)S(1)}, bf16[144,640]{1,0:T(8,128)(2,1)S(1)}, u32[]{:S(2)}, u32[]{:S(2)}) collective-permute-start(bf16[144,640]{1,0:T(8,128)(2,1)S(1)} %get-tuple-element.59), channel_id=1, source_target_pairs={{0,16},{8,24},{16,32},{24,40},{32,48},{40,56},{48,0},{56,8},{64,80... | collective-permute-start | bytes 552968 | tf_op jit(solution)/shard_map/ppermute | solution.py:565
  90.0 14.2 %collective-permute-start.17 = (bf16[96,640]{1,0:T(8,128)(2,1)S(1)}, bf16[96,640]{1,0:T(8,128)(2,1)S(1)}, u32[]{:S(2)}, u32[]{:S(2)}) collective-permute-start(bf16[96,640]{1,0:T(8,128)(2,1)S(1)} %get-tuple-element.60), channel_id=1, source_target_pairs={{0,48},{8,56},{16,0},{24,8},{32,16},{40,24},{48,32},{56,40},{64,11... | collective-permute-start | bytes 368648 | tf_op jit(solution)/shard_map/ppermute | solution.py:565
  92.5 12.1 %collective-permute-start.16 = (bf16[96,640]{1,0:T(8,128)(2,1)S(1)}, bf16[96,640]{1,0:T(8,128)(2,1)S(1)}, u32[]{:S(2)}, u32[]{:S(2)}) collective-permute-start(bf16[96,640]{1,0:T(8,128)(2,1)S(1)} %get-tuple-element.62), channel_id=1, source_target_pairs={{0,16},{8,24},{16,32},{24,40},{32,48},{40,56},{48,0},{56,8},{64,80... | collective-permute-start | bytes 368648 | tf_op jit(solution)/shard_map/ppermute | solution.py:565
  102.9 15.4 %collective-permute-start.15 = (bf16[3,40,640]{2,1,0:T(8,128)(2,1)S(1)}, bf16[3,40,640]{2,1,0:T(8,128)(2,1)S(1)}, u32[]{:S(2)}, u32[]{:S(2)}) collective-permute-start(bf16[3,40,640]{2,1,0:T(8,128)(2,1)S(1)} %get-tuple-element.51), channel_id=1, source_target_pairs={{64,0},{72,8},{80,16},{88,24},{96,32},{104,40},{112,48},{120,56},{... | collective-permute-start | bytes 460808 | tf_op jit(solution)/shard_map/ppermute | solution.py:565

commit v2 on v1

--- a/solution.py
+++ b/solution.py
@@ -142,7 +142,8 @@
 EARLY = Chunk("early", ((0, 0, 40), (1, 0, 8)))
 LATE = Chunk("late", ((1, 8, 32),))
 CHUNKS = (EARLY, LATE)
-UNITS = EARLY.rows + LATE.rows
+OWNED = EARLY.span + LATE.span
+UNITS = RING * OWNED
 
 
 def factors(gate_pre, up_pre, back, rate_ref, x_ref, at):
@@ -194,49 +195,40 @@
             copy.wait()
 
 
-def contract(x_ref, keys_ref, values_ref, outs):
+def piece_rows():
+    at = 0
+    for chunk, lo in zip(CHUNKS, (0, EARLY.span)):
+        for m in range(3):
+            yield m, lo, at + m * chunk.span, chunk.span
+        at += 3 * chunk.span
+
+
+def contract(x_ref, keys_ref, values_ref, out_ref):
     for m in range(3):
-        right = (values_ref if m == 2 else keys_ref)[...]
-        term = dot(x_ref[m], right, NN)
-        base = 0
-        for chunk, (mine_ref, theirs_ref) in zip(CHUNKS, outs):
-            span = chunk.span
-            for d in range(RING):
-                for e, ref in enumerate((mine_ref, theirs_ref)):
-                    at = base + span * (2 * d + e)
-                    ref[d, m * span : (m + 1) * span] = term[at : at + span].astype(BF16)
-            base += chunk.rows
-
-
-def order_rows(info_ref, raw_ref, w_ref, m):
+        term = dot(x_ref[m], (values_ref if m == 2 else keys_ref)[...], NN)
+        for d in range(RING):
+            for matrix, lo, at, n in piece_rows():
+                if matrix == m:
+                    here = d * OWNED + lo
+                    out_ref[d, at : at + n] = term[here : here + n].astype(BF16)
+
+
+def order_rows(info_ref, raw_ref, w_ref, m, other):
     half = raw_ref.shape[1] // 2
     owned = half // SLOTS
     z, c = info_ref[2], info_ref[3]
-    base = 0
-    for chunk in CHUNKS:
-        for d in range(RING):
-            for e in range(2):
-                owner = 2 * lax.rem(z + d, RING) + (c if e == 0 else 1 - c)
-                rows = [
-                    raw_ref[m, pl.ds(pl.multiple_of(owner * owned + h * half + lo, 8), n)]
-                    for h, lo, n in chunk.spans
-                ]
-                w_ref[m, base : base + chunk.span] = jnp.concatenate(rows, 0).astype(BF16)
-                base += chunk.span
+    for d in range(RING):
+        owner = 2 * lax.rem(z + d, RING) + (1 - c if other else c)
+        first = pl.multiple_of(owner * owned, 8)
+        rows = [raw_ref[m, pl.ds(first, owned)], raw_ref[m, pl.ds(first + half, owned)]]
+        w_ref[m, d * OWNED : (d + 1) * OWNED] = jnp.concatenate(rows, 0).astype(BF16)
 
 
 def fill_gathered(sources, w_ref):
-    base, at = 0, 0
-    for chunk in CHUNKS:
-        for d in range(RING):
-            for e in range(2):
-                from_there = (-d) % RING
-                ref = sources[RING].at[from_there] if e else sources[from_there]
-                for m in range(3):
-                    here = at + m * chunk.span
-                    w_ref[m, base : base + chunk.span] = ref[here : here + chunk.span]
-                base += chunk.span
-        at += 3 * chunk.span
+    for d in range(RING):
+        for m, lo, at, n in piece_rows():
+            here = d * OWNED + lo
+            w_ref[m, here : here + n] = sources[(-d) % RING][at : at + n]
 
 
 HERE = pl.BlockSpec(memory_space=pltpu.VMEM)
@@ -278,121 +270,106 @@
     )(info, *sources)
 
 
-def piece_shapes(width, chunked):
-    heights = (SPLIT, PIECE - SPLIT) if chunked else (PIECE,)
-    return [
-        jax.ShapeDtypeStruct((RING, height, width), BF16) for height in heights for _ in range(2)
-    ]
-
-
-def gradient_first(info, initial, keys, values, rates):
-    rows, width = keys.shape
-
-    def body(info_ref, raw_ref, key_hbm, value_hbm, rate_ref, mine, theirs, w_out, *refs):
-        w_ref, x_ref, ks_ref, vs_ref, save_sem, t_sems = refs
-
-        @pl.when(info_ref[1] == 0)
+def gradient_call(name, block, other, fill, info, sources, staged, rates, kept=None, tokens=()):
+    width = sources[0].shape[-1]
+    rows = rates.shape[1]
+    first = len(tokens) > 0
+    count = len(sources)
+    extra = [] if kept is None else [kept]
+    held = list(tokens) if first else [staged]
+    row0 = UNITS if other else 0
+
+    def body(info_ref, *refs):
+        source_refs, refs = refs[:count], refs[count:]
+        held_refs, refs = refs[: len(held)], refs[len(held) :]
+        rate_ref, refs = refs[0], refs[1 + len(extra) :]
+        out_ref, w_out, *refs = refs
+        if first:
+            staged_ref, w_ref, x_ref, save_sem, t_sems = refs
+        else:
+            staged_ref = held_refs[0]
+            w_ref, x_ref, save_sem = refs
+        keys_ref, values_ref = staged_ref.at[0], staged_ref.at[1]
+        save = pltpu.make_async_copy(w_ref, w_out.at[:, pl.ds(row0, UNITS)], save_sem)
+        steps = rows // TILE
+        if first:
+            arriving = Tokens(*held_refs, keys_ref, values_ref, t_sems)
+
+            @pl.when(info_ref[1] != block)
+            def _():
+                for t in range(steps):
+                    arriving.start(t)
+                for t in range(steps):
+                    arriving.wait(t)
+
+        @pl.when(info_ref[1] == block)
         def _():
-            tokens = Tokens(key_hbm, value_hbm, ks_ref, vs_ref, t_sems)
-            save = pltpu.make_async_copy(w_ref, w_out, save_sem)
-            first_keys, first_values = tokens.copies(0)
-            first_keys.start()
-            first_values.start()
-            tokens.start(1)
-            pre = []
-            at = pl.ds(0, TILE)
-            for m in range(3):
-                order_rows(info_ref, raw_ref, w_ref, m)
-                if m == 0:
-                    first_keys.wait()
-                if m == 2:
-                    first_values.wait()
-                pre.append(dot(w_ref[m], (vs_ref if m == 2 else ks_ref)[at], NT))
-            factors(*pre, rate_ref, x_ref, at)
+            if first:
+                arriving.start(0)
+            fill(info_ref, source_refs, w_ref)
 
             def one_tile(t, carry):
-                @pl.when(t + 1 < tokens.count)
-                def _():
-                    tokens.start(t + 1)
-
-                tokens.wait(t)
-                tile_factors(w_ref, ks_ref, vs_ref, rate_ref, x_ref, tokens.at(t))
-                return carry
-
-            lax.fori_loop(1, tokens.count, one_tile, 0)
-            save.start()
-            halves = [
-                [ref.at[:, at] for ref in (mine, theirs)]
-                for at in (slice(0, SPLIT), slice(SPLIT, PIECE))
-            ]
-            contract(x_ref, ks_ref, vs_ref, halves)
-            save.wait()
-
-    return pl.pallas_call(
-        body,
-        out_shape=piece_shapes(width, False) + [jax.ShapeDtypeStruct((3, UNITS, width), BF16)],
-        grid_spec=pltpu.PrefetchScalarGridSpec(
-            num_scalar_prefetch=1,
-            grid=(1,),
-            in_specs=[HERE] + [ANYWHERE] * 2 + [pl.BlockSpec(rates.shape, lambda i, s: (0, 0))],
-            out_specs=[HERE] * 2 + [ANYWHERE],
-            scratch_shapes=[
-                pltpu.VMEM((3, UNITS, width), BF16),
-                pltpu.VMEM((3, UNITS, rows), BF16),
-                pltpu.VMEM((rows, width), BF16),
-                pltpu.VMEM((rows, width), BF16),
-                pltpu.SemaphoreType.DMA(()),
-                pltpu.SemaphoreType.DMA((2, rows // TILE)),
-            ],
-        ),
-        compiler_params=params(),
-        name="gradient_first",
-    )(info, initial, keys, values, rates)
-
-
-def gradient_second(info, gathered, staged, rates, kept):
-    _, rows, width = staged.shape
-    count = RING + 1
-
-    def body(info_ref, *refs):
-        sources, refs = refs[:count], refs[count:]
-        staged_ref, rate_ref, _, ma, ta, mb, tb, w_out, w_ref, x_ref, save_sem = refs
-        keys_ref, values_ref = staged_ref.at[0], staged_ref.at[1]
-
-        @pl.when(info_ref[1] == 1)
-        def _():
-            fill_gathered(sources, w_ref)
-            save = pltpu.make_async_copy(w_ref, w_out, save_sem)
-
-            def one_tile(t, carry):
+                if first:
+
+                    @pl.when(t + 1 < steps)
+                    def _():
+                        arriving.start(t + 1)
+
+                    arriving.wait(t)
                 at = pl.ds(pl.multiple_of(t * TILE, TILE), TILE)
                 tile_factors(w_ref, keys_ref, values_ref, rate_ref, x_ref, at)
                 return carry
 
-            lax.fori_loop(0, rows // TILE, one_tile, 0)
+            lax.fori_loop(0, steps, one_tile, 0)
             save.start()
-            contract(x_ref, keys_ref, values_ref, ((ma, ta), (mb, tb)))
+            contract(x_ref, keys_ref, values_ref, out_ref)
             save.wait()
 
-    return pl.pallas_call(
-        body,
-        out_shape=piece_shapes(width, True) + [jax.ShapeDtypeStruct(kept.shape, BF16)],
+    shapes = [
+        jax.ShapeDtypeStruct((RING, PIECE, width), BF16),
+        jax.ShapeDtypeStruct((3, 2 * UNITS, width), BF16),
+    ]
+    scratch = [
+        pltpu.VMEM((3, UNITS, width), BF16),
+        pltpu.VMEM((3, UNITS, rows), BF16),
+        pltpu.SemaphoreType.DMA(()),
+    ]
+    if first:
+        shapes.append(jax.ShapeDtypeStruct((2, rows, width), BF16))
+        scratch.append(pltpu.SemaphoreType.DMA((2, rows // TILE)))
+    return pl.pallas_call(
+        body,
+        out_shape=shapes,
         grid_spec=pltpu.PrefetchScalarGridSpec(
             num_scalar_prefetch=1,
             grid=(1,),
-            in_specs=[HERE] * (count + 1)
-            + [pl.BlockSpec(rates.shape, lambda i, s: (0, 0)), ANYWHERE],
-            out_specs=[HERE] * 4 + [ANYWHERE],
-            scratch_shapes=[
-                pltpu.VMEM((3, UNITS, width), BF16),
-                pltpu.VMEM((3, UNITS, rows), BF16),
-                pltpu.SemaphoreType.DMA(()),
-            ],
-        ),
-        input_output_aliases={count + 3: 4},
+            in_specs=[HERE] * count
+            + [ANYWHERE if first else HERE] * len(held)
+            + [pl.BlockSpec(rates.shape, lambda i, s: (0, 0))]
+            + [ANYWHERE] * len(extra),
+            out_specs=[HERE, ANYWHERE] + [HERE] * (len(shapes) - 2),
+            scratch_shapes=scratch,
+        ),
+        input_output_aliases={count + len(held) + 2: 1} if extra else {},
         compiler_params=params(30),
-        name="gradient_second",
-    )(info, *gathered, staged, rates, kept)
+        name=name,
+    )(info, *sources, *held, rates, *extra)
+
+
+def fill_initial(other):
+    def fill(info_ref, source_refs, w_ref):
+        for m in range(3):
+            order_rows(info_ref, source_refs[0], w_ref, m, other)
+
+    return fill
+
+
+def fill_column(info_ref, source_refs, w_ref):
+    fill_gathered(source_refs, w_ref)
+
+
+def fill_beside(info_ref, source_refs, w_ref):
+    fill_gathered([source_refs[0].at[d] for d in range(RING)], w_ref)
 
 
 def fast_apply(info, queries, weights, gain, attended, tile=512):
@@ -436,8 +413,8 @@
     return moved * (jnp.sqrt(size) / jnp.sqrt(moved_size))
 
 
-def total(mine_ref, other_ref, *arrived):
-    out = mine_ref[0].astype(F32) + other_ref[0].astype(F32)
+def total(mine_ref, other_ref, at, *arrived):
+    out = mine_ref[0, at].astype(F32) + other_ref[0, at].astype(F32)
     for ref in arrived:
         out = out + ref[...].astype(F32)
     return out
@@ -453,7 +430,7 @@
         )
 
     def body(info_ref, mine_ref, other_ref, a_ref, b_ref, c_ref, w0_ref, w1_ref, cast_ref, keep_ref):
-        gradient = total(mine_ref, other_ref, a_ref, b_ref, c_ref)
+        gradient = total(mine_ref, other_ref, slice(0, PIECE), a_ref, b_ref, c_ref)
         base = 0
         for chunk in CHUNKS:
             for m in range(3):
@@ -483,7 +460,7 @@
 
 
 def sum_body(mine_ref, other_ref, a_ref, b_ref, both_ref, near_ref, far_ref):
-    gradient = total(mine_ref, other_ref, a_ref, b_ref, both_ref.at[:SPLIT])
+    gradient = total(mine_ref, other_ref, slice(0, SPLIT), a_ref, b_ref, both_ref.at[:SPLIT])
     owned, rest = near_ref.shape[1], far_ref.shape[1]
     for m in range(3):
         at = m * (owned + rest)
@@ -492,13 +469,13 @@
 
 
 def sum_call(mine, other, arrived):
-    _, span3, width = mine.shape
+    width = mine.shape[2]
     owned = EARLY.spans[0][2]
     return pl.pallas_call(
         sum_body,
         out_shape=(
             jax.ShapeDtypeStruct((3, owned, width), BF16),
-            jax.ShapeDtypeStruct((3, span3 // 3 - owned, width), F32),
+            jax.ShapeDtypeStruct((3, EARLY.span - owned, width), F32),
         ),
         in_specs=[HERE] * 5,
         out_specs=[HERE] * 2,
@@ -508,7 +485,7 @@
 
 
 def final_far(info, mine, other, arrived, cast, far):
-    shape = (3, EARLY.spans[0][2], cast.shape[1])
+    shape = (3, EARLY.spans[0][2], cast.shape[2])
 
     def body(info_ref, mine_ref, other_ref, a_ref, b_ref, both_ref, cast_ref, far_ref, o_ref):
         rest = far_ref.shape[1]
@@ -516,14 +493,15 @@
 
         @pl.when(info_ref[1] == 1)
         def _():
-            gradient = total(mine_ref, other_ref, a_ref, b_ref, both_ref.at[SPLIT:])
+            late = slice(SPLIT, PIECE)
+            gradient = total(mine_ref, other_ref, late, a_ref, b_ref, both_ref.at[SPLIT:])
             for m in range(3):
                 at = m * EARLY.span
-                early = cast_ref[at : at + EARLY.span].astype(F32)[owned:]
+                early = cast_ref[0, at : at + EARLY.span].astype(F32)[owned:]
                 o_ref[m, :rest] = renormalize(early, far_ref[m])
                 at = m * LATE.span
-                late = cast_ref[SPLIT + at : SPLIT + at + LATE.span].astype(F32)
-                o_ref[m, rest:] = renormalize(late, gradient[at : at + LATE.span])
+                old = cast_ref[0, SPLIT + at : SPLIT + at + LATE.span].astype(F32)
+                o_ref[m, rest:] = renormalize(old, gradient[at : at + LATE.span])
 
     return pl.pallas_call(
         body,
@@ -575,7 +553,7 @@
 
 
 SIBLING = [(k, k ^ 1) for k in range(16)]
-ACROSS = [(k, k + 8) for k in range(8)]
+ACROSS = [(k, (k ^ 1) + 8) for k in range(8)]
 BACK = [(k + 8, k) for k in range(8)]
 
 
@@ -587,10 +565,8 @@
     return lax.optimization_barrier((x, *others))[0]
 
 
-def joined(mine, other):
-    return [
-        (mine[d].astype(F32) + other[d].astype(F32)).astype(BF16) for d in range(1, RING)
-    ]
+def joined(mine, other, at=slice(0, PIECE), places=range(1, RING)):
+    return [(mine[d, at].astype(F32) + other[d, at].astype(F32)).astype(BF16) for d in places]
 
 
 def around(pieces):
@@ -610,9 +586,16 @@
     onward = [(i, (i + 1) % 16) for i in range(16)]
     tails = fetch(info, attn[1:], WINDOW)
 
-    mine, theirs, weights = gradient_first(after(info, tails), initial, *tokens)
+    theirs, weights, staged = gradient_call(
+        "first_theirs", 0, True, fill_initial(True), after(info, tails), [initial], None,
+        tokens[2], tokens=tokens[:2],
+    )
     halo = send(tails, onward)
     other = send(theirs, SIBLING)
+    mine, weights = gradient_call(
+        "first_mine", 0, False, fill_initial(False), after(info, theirs), [initial], staged,
+        tokens[2], weights,
+    )
     parts = joined(after(mine, halo), other)
     ring = around(parts)
     attended = attention_rest(after(info, *parts), *attn, 1)
@@ -620,27 +603,31 @@
     own = send(cast, ACROSS)
     attended = attention_rest(after(info, cast), *attn, 0, attended)
 
-    staged = fetch(after(info, attended), tokens[:2], row_count)
-    own = after(own, staged)
+    own = after(own, attended)
     ring = around([own] * (RING - 1))
-    attended = attention_first(after(info, own, staged), *attn, halo, attended)
+    attended = attention_first(after(info, own), *attn, halo, attended)
     column = [own] + [after(piece, attended) for piece in ring]
     beside = send(jnp.stack(column), SIBLING)
-    mine_a, theirs_a, mine_b, theirs_b, weights = gradient_second(
-        info, [*column, beside], staged, tokens[2], weights
+    theirs, weights = gradient_call(
+        "second_theirs", 1, True, fill_column, info, column, staged, tokens[2], weights
     )
-    other_a = send(theirs_a, SIBLING)
-    other_b = send(theirs_b, SIBLING)
-    part_a = joined(mine_a, other_a)
-    part_b = joined(mine_b, other_b)
-    both = jnp.concatenate([part_a[1], part_b[1]], 0)
-    ring_a = [send(part_a[0], along_z(1)), send(part_a[2], along_z(3))]
-    ring_b = [send(part_b[0], along_z(1)), send(part_b[2], along_z(3))]
-    both = send(both, along_z(2))
-    mixed = fast_apply(after(info, *part_a, *part_b), fast_query, weights, gain, attended)
-    near, far = sum_call(after(mine_a, mixed), other_a, [*ring_a, both])
+    other = send(theirs, SIBLING)
+    mine, weights = gradient_call(
+        "second_mine", 1, False, fill_beside, after(info, theirs), [beside], staged, tokens[2],
+        weights,
+    )
+    early, late = slice(0, SPLIT), slice(SPLIT, PIECE)
+    part_a = joined(mine, other, early, (1, 3))
+    part_b = joined(mine, other, late, (1, 3))
+    (both,) = joined(mine, other, places=(2,))
+    ring_a = [send(part, along_z(d)) for part, d in zip(part_a, (1, 3))]
+    ring_b = [send(part, along_z(d)) for part, d in zip(part_b, (1, 3))]
+    both_there = send(both, along_z(2))
+    ready = after(info, both, *part_a, *part_b)
+    mixed = fast_apply(ready, fast_query, weights, gain, attended)
+    near, far = sum_call(after(mine, mixed), other, [*ring_a, both_there])
     near = send(near, BACK)
-    far_rows = final_far(after(info, far), mine_b, other_b, [*ring_b, both], own, far)
+    far_rows = final_far(after(info, far), mine, other, [*ring_b, both_there], beside, far)
     final = final_near(info, middle, near, far_rows)
     return mixed, jnp.transpose(final, (1, 0, 2))[None]
 

time: 120 us -> 117 us (0.975)
  waiting for transfers between devices: 45.4 us -> 41.5 us
    ppermute x18 -> x17, waiting for transfers between devices: 45.4 us -> 41.5 us  [send(): return lax.ppermute(x, 'seq', pairs)]
    pallas_call x2 -> x4, Pallas kernels: 18.3 us -> 22.1 us  [gradient_call(): pl.pallas_call(body, out_shape=shapes, grid_spec=pltpu.PrefetchScalarGrid...]
    pallas_call x2 -> x1, Pallas kernels: 5.2 us -> 2.11 us  [fetch(): pl.pallas_call(body, out_shape=jax.ShapeDtypeStruct((len(sources), height...]
    ppermute x18 -> x17, starting transfers between devices: 17.5 us -> 17.8 us  [send(): return lax.ppermute(x, 'seq', pairs)]
  transfers between devices with their start and end apart: 18 -> 17, of which waited for: 11 -> 8; matrix products, arithmetic and copies ran while one was open for 0% -> 0% of each run, Pallas kernels for 41% -> 44%
where the time goes in v2:
time: 117 us
  Pallas kernels  55.3 us (47%)
  waiting for transfers between devices  41.5 us (35%)
  starting transfers between devices  17.8 us (15%)
    ppermute x17, waiting for transfers between devices, send(): return lax.ppermute(x, 'seq', pairs)  41.5 us
    pallas_call x4, Pallas kernels, gradient_call(): pl.pallas_call(body, out_shape=shapes, grid_spec=pltpu.PrefetchScalarGrid...  22.1 us
    ppermute x17, starting transfers between devices, send(): return lax.ppermute(x, 'seq', pairs)  17.8 us
    pallas_call x2, Pallas kernels, attention_rest(): pl.pallas_call(body, out_shape=jax.ShapeDtypeStruct((rows, width), F32),...  13.2 us
    pallas_call x1, Pallas kernels, fast_apply(): pl.pallas_call(body, out_shape=jax.ShapeDtypeStruct((rows, width), BF16),...  10.3 us
    pallas_call x1, Pallas kernels, attention_first(): pl.pallas_call(body, out_shape=jax.ShapeDtypeStruct((rows, width), F32),...  4.61 us
  transfers between devices with their start and end apart: 17, of which 8 were waited for; matrix products, arithmetic and copies ran while one was open for 0% of the time, Pallas kernels for 44%

profile of v2, /device:TPU:0, one launch (start us, length us, event | category | flops | bytes accessed | tf_op | source)
XLA Modules:
  0.0 116.7 jit_solution(7718843144442056456)
XLA Ops:
  0.8 2.1 %fetch.1 = bf16[2,512,640]{2,1,0:T(8,128)(2,1)S(1)} custom-call(s32[4]{0:T(128)S(1)} %pad_add_fusion.info_ref, bf16[2048,640]{1,0:T(8,128)(2,1)} %kc_ref.5, bf16[2048,640]{1,0:T(8,128)(2,1)} %vc_ref.5), custom_call_target="tpu_custom_call" | custom-call | tf_op jit(solution)/shard_map/fetch/pallas_call | solution.py:258
  3.5 10.5 %first_theirs.1 = (bf16[4,240,640]{2,1,0:T(8,128)(2,1)S(1)}, bf16[3,640,640]{2,1,0:T(8,128)(2,1)S(1)}, bf16[2,2048,640]{2,1,0:T(8,128)(2,1)S(1)}) custom-call(s32[4]{0:T(128)S(1)} %pad_add_fusion.info_ref, f32[3,640,640]{2,1,0:T(8,128)S(1)} %bitcast.31, bf16[2048,640]{1,0:T(8,128)(2,1)} %refs_1_.3, bf16[2048,640]{1,0:T(8,128)(2,1)} %refs_2_.1, ...), custom_call_target="tpu_custom_call" | custom-call | tf_op jit(solution)/shard_map/first_theirs/pallas_call | solution.py:340
  14.1 1.6 %collective-permute-start.1 = (bf16[4,240,640]{2,1,0:T(8,128)(2,1)S(1)}, bf16[4,240,640]{2,1,0:T(8,128)(2,1)S(1)}, u32[]{:S(2)}, u32[]{:S(2)}) collective-permute-start(bf16[4,240,640]{2,1,0:T(8,128)(2,1)S(1)} %get-tuple-element.31), channel_id=1, source_target_pairs={{0,8},{8,0},{16,24},{24,16},{32,40},{40,32},{48,56},{56,48},{64,72... | collective-permute-start | bytes 3686408 | tf_op jit(solution)/shard_map/ppermute | solution.py:543
  15.7 9.0 %first_mine.1 = (bf16[4,240,640]{2,1,0:T(8,128)(2,1)S(1)}, bf16[3,640,640]{2,1,0:T(8,128)(2,1)S(1)}) custom-call(s32[4]{0:T(128)S(1)} %pad_add_fusion.info_ref, f32[3,640,640]{2,1,0:T(8,128)S(1)} %bitcast.32, bf16[2,2048,640]{2,1,0:T(8,128)(2,1)S(1)} %get-tuple-element.33.refs_1_.refs_4_, f32[1,2048]{1,0:T(1,128)} %bitcast.41, ...), custom_call_target="tpu_custom_call", output_to_operand_aliasing={{1}: (4, {})} | custom-call | tf_op jit(solution)/shard_map/first_mine/pallas_call | solution.py:340
  25.0 4.0 %collective-permute-start.4 = (bf16[240,640]{1,0:T(8,128)(2,1)S(1)}, bf16[240,640]{1,0:T(8,128)(2,1)S(1)}, u32[]{:S(2)}, u32[]{:S(2)}) collective-permute-start(bf16[240,640]{1,0:T(8,128)(2,1)S(1)} %get-tuple-element.62), channel_id=1, source_target_pairs={{0,48},{8,56},{16,0},{24,8},{32,16},{40,24},{48,32},{56,40},{64,11... | collective-permute-start | bytes 921608 | tf_op jit(solution)/shard_map/ppermute | solution.py:543
  29.0 1.0 collective-permute-start.2
  30.0 2.4 %attention_rest_1.1.rest_0_ = f32[2048,640]{1,0:T(8,128)S(1)} custom-call(s32[4]{0:T(128)S(1)} %pad_add_fusion.info_ref, bf16[2048,640]{1,0:T(8,128)(2,1)} %q_ref.6, bf16[2048,640]{1,0:T(8,128)(2,1)} %kc_ref.5, bf16[2048,640]{1,0:T(8,128)(2,1)} %kc_ref.5, bf16[2048,640]{1,0:T(8,128)(2,1)} %vc_ref.5, bf16[2048,640]{1,0:T(8,128)(2,1)} %vc_ref.5), custom_call_target="tpu_custom_call" | custom-call | tf_op jit(solution)/shard_map/attention_rest_1/pallas_call | solution.py:114
  32.5 9.8 %collective-permute-done.4.c_ref = bf16[240,640]{1,0:T(8,128)(2,1)S(1)} collective-permute-done((bf16[240,640]{1,0:T(8,128)(2,1)S(1)}, bf16[240,640]{1,0:T(8,128)(2,1)S(1)}, u32[]{:S(2)}, u32[]{:S(2)}) %collective-permute-start.4) | collective-permute-done | bytes 307232 | tf_op jit(solution)/shard_map/ppermute | solution.py:543
  42.3 3.4 %collective-permute-done.2.a_ref = bf16[240,640]{1,0:T(8,128)(2,1)S(1)} collective-permute-done((bf16[240,640]{1,0:T(8,128)(2,1)S(1)}, bf16[240,640]{1,0:T(8,128)(2,1)S(1)}, u32[]{:S(2)}, u32[]{:S(2)}) %collective-permute-start.2) | collective-permute-done | bytes 307232 | tf_op jit(solution)/shard_map/ppermute | solution.py:543
  46.6 1.5 %collective-permute-start.5 = (bf16[240,640]{1,0:T(8,128)(2,1)S(1)}, bf16[240,640]{1,0:T(8,128)(2,1)S(1)}, u32[]{:S(2)}, u32[]{:S(2)}) collective-permute-start(bf16[240,640]{1,0:T(8,128)(2,1)S(1)} %get-tuple-element.39), channel_id=1, source_target_pairs={{0,72},{8,64},{16,88},{24,80},{32,104},{40,96},{48,120},{56,112},{... | collective-permute-start | bytes 921608 | tf_op jit(solution)/shard_map/ppermute | solution.py:543
  48.1 10.7 %attention_rest_0.1._ = f32[2048,640]{1,0:T(8,128)S(1)} custom-call(s32[4]{0:T(128)S(1)} %pad_add_fusion.info_ref, bf16[2048,640]{1,0:T(8,128)(2,1)} %q_ref.6, bf16[2048,640]{1,0:T(8,128)(2,1)} %kc_ref.5, bf16[2048,640]{1,0:T(8,128)(2,1)} %kc_ref.5, bf16[2048,640]{1,0:T(8,128)(2,1)} %vc_ref.5, ...), custom_call_target="tpu_custom_call", output_to_operand_aliasing={{}: (6, {})} | custom-call | tf_op jit(solution)/shard_map/attention_rest_0/pallas_call | solution.py:114
  61.0 4.6 %attention_first.1.att_ref = f32[2048,640]{1,0:T(8,128)S(1)} custom-call(s32[4]{0:T(128)S(1)} %pad_add_fusion.info_ref, bf16[2048,640]{1,0:T(8,128)(2,1)} %q_ref.6, bf16[2,512,640]{2,1,0:T(8,128)(2,1)S(1)} %collective-permute-done.kp_ref.vp_ref, bf16[2048,640]{1,0:T(8,128)(2,1)} %kc_ref.5, ...), custom_call_target="tpu_custom_call", output_to_operand_aliasing={{}: (6, {})} | custom-call | tf_op jit(solution)/shard_map/attention_first/pallas_call | solution.py:79
  65.6 3.5 %collective-permute-done.8.refs_3_ = bf16[240,640]{1,0:T(8,128)(2,1)S(1)} collective-permute-done((bf16[240,640]{1,0:T(8,128)(2,1)S(1)}, bf16[240,640]{1,0:T(8,128)(2,1)S(1)}, u32[]{:S(2)}, u32[]{:S(2)}) %collective-permute-start.8) | collective-permute-done | bytes 307232 | tf_op jit(solution)/shard_map/ppermute | solution.py:543
  69.1 2.5 %collective-permute-done.7.refs_2_ = bf16[240,640]{1,0:T(8,128)(2,1)S(1)} collective-permute-done((bf16[240,640]{1,0:T(8,128)(2,1)S(1)}, bf16[240,640]{1,0:T(8,128)(2,1)S(1)}, u32[]{:S(2)}, u32[]{:S(2)}) %collective-permute-start.7) | collective-permute-done | bytes 307232 | tf_op jit(solution)/shard_map/ppermute | solution.py:543
  71.6 4.4 %collective-permute-done.6.refs_1_ = bf16[240,640]{1,0:T(8,128)(2,1)S(1)} collective-permute-done((bf16[240,640]{1,0:T(8,128)(2,1)S(1)}, bf16[240,640]{1,0:T(8,128)(2,1)S(1)}, u32[]{:S(2)}, u32[]{:S(2)}) %collective-permute-start.6) | collective-permute-done | bytes 307232 | tf_op jit(solution)/shard_map/ppermute | solution.py:543
  76.3 1.2 %second_theirs.1 = (bf16[4,240,640]{2,1,0:T(8,128)(2,1)S(1)}, bf16[3,640,640]{2,1,0:T(8,128)(2,1)S(1)}) custom-call(s32[4]{0:T(128)S(1)} %pad_add_fusion.info_ref, bf16[240,640]{1,0:T(8,128)(2,1)S(1)} %collective-permute-done.5.refs_0_, bf16[240,640]{1,0:T(8,128)(2,1)S(1)} %collective-permute-done.6.refs_1_, ...), custom_call_target="tpu_custom_call", output_to_operand_aliasing={{1}: (7, {})} | custom-call | tf_op jit(solution)/shard_map/second_theirs/pallas_call | solution.py:340
  78.1 1.1 collective-permute-done.9.refs_0_.cast_ref
  79.2 1.2 %second_mine.1 = (bf16[4,240,640]{2,1,0:T(8,128)(2,1)S(1)}, bf16[3,640,640]{2,1,0:T(8,128)(2,1)S(1)}) custom-call(s32[4]{0:T(128)S(1)} %pad_add_fusion.info_ref, bf16[4,240,640]{2,1,0:T(8,128)(2,1)S(1)} %collective-permute-done.9.refs_0_.cast_ref, bf16[2,2048,640]{2,1,0:T(8,128)(2,1)S(1)} %get-tuple-element.33.refs_1_.refs_4_, ...), custom_call_target="tpu_custom_call", output_to_operand_aliasing={{1}: (4, {})} | custom-call | tf_op jit(solution)/shard_map/second_mine/pallas_call | solution.py:340
  82.1 1.3 %collective-permute-start.12 = (bf16[144,640]{1,0:T(8,128)(2,1)S(1)}, bf16[144,640]{1,0:T(8,128)(2,1)S(1)}, u32[]{:S(2)}, u32[]{:S(2)}) collective-permute-start(bf16[144,640]{1,0:T(8,128)(2,1)S(1)} %get-tuple-element.60), channel_id=1, source_target_pairs={{0,48},{8,56},{16,0},{24,8},{32,16},{40,24},{48,32},{56,40},{64,11... | collective-permute-start | bytes 552968 | tf_op jit(solution)/shard_map/ppermute | solution.py:543
  84.3 2.5 %collective-permute-start.16 = (bf16[96,640]{1,0:T(8,128)(2,1)S(1)}, bf16[96,640]{1,0:T(8,128)(2,1)S(1)}, u32[]{:S(2)}, u32[]{:S(2)}) collective-permute-start(bf16[96,640]{1,0:T(8,128)(2,1)S(1)} %get-tuple-element.58), channel_id=1, source_target_pairs={{0,48},{8,56},{16,0},{24,8},{32,16},{40,24},{48,32},{56,40},{64,11... | collective-permute-start | bytes 368648 | tf_op jit(solution)/shard_map/ppermute | solution.py:543
  86.8 10.3 %fast_apply.1 = bf16[2048,640]{1,0:T(8,128)(2,1)} custom-call(s32[4]{0:T(128)S(1)} %pad_add_fusion.info_ref, bf16[2048,640]{1,0:T(8,128)(2,1)S(1)} %copy-done.1, bf16[3,640,640]{2,1,0:T(8,128)(2,1)S(1)} %get-tuple-element.52.w_ref, f32[1,640]{1,0:T(1,128)S(1)} %copy-done.2, f32[2048,640]{1,0:T(8,128)S(1)} %attention_first.1.att_ref), custom_call_target="tpu_custom_call" | custom-call | tf_op jit(solution)/shard_map/fast_apply/pallas_call | solution.py:388
  97.2 1.3 %collective-permute-start.14 = (bf16[3,40,640]{2,1,0:T(8,128)(2,1)S(1)}, bf16[3,40,640]{2,1,0:T(8,128)(2,1)S(1)}, u32[]{:S(2)}, u32[]{:S(2)}) collective-permute-start(bf16[3,40,640]{2,1,0:T(8,128)(2,1)S(1)} %get-tuple-element.55), channel_id=1, source_target_pairs={{64,0},{72,8},{80,16},{88,24},{96,32},{104,40},{112,48},{120,56},{... | collective-permute-start | bytes 460808 | tf_op jit(solution)/shard_map/ppermute | solution.py:543
  99.1 16.2 %collective-permute-done.14.near_ref = bf16[3,40,640]{2,1,0:T(8,128)(2,1)S(1)} collective-permute-done((bf16[3,40,640]{2,1,0:T(8,128)(2,1)S(1)}, bf16[3,40,640]{2,1,0:T(8,128)(2,1)S(1)}, u32[]{:S(2)}, u32[]{:S(2)}) %collective-permute-start.14) | collective-permute-done | bytes 153632 | tf_op jit(solution)/shard_map/ppermute | solution.py:543
  115.3 1.4 %final_near.1 = f32[3,40,640]{2,1,0:T(8,128)} custom-call(s32[4]{0:T(128)S(1)} %pad_add_fusion.info_ref, f32[3,40,640]{2,1,0:T(8,128)S(1)} %get-tuple-element.53.middle_ref, bf16[3,40,640]{2,1,0:T(8,128)(2,1)S(1)} %collective-permute-done.14.near_ref, f32[3,40,640]{2,1,0:T(8,128)S(1)} %final_far.1.far_ref), custom_call_target="tpu_custom_call" | custom-call | tf_op jit(solution)/shard_map/final_near/pallas_call | solution.py:531
  (35 shorter events, 8.1 us)
Async XLA Ops:
  0.8 2.8 %copy-start = (f32[1,640,3,640]{3,1,2,0:T(8,128)S(1)}, f32[1,640,3,640]{3,1,2,0:T(8,128)}, u32[]{:S(2)}) copy-start(f32[1,640,3,640]{3,1,2,0:T(8,128)} %param.16) | copy-start | bytes 14745604
  2.9 21.8 %collective-permute-start = (bf16[2,512,640]{2,1,0:T(8,128)(2,1)S(1)}, bf16[2,512,640]{2,1,0:T(8,128)(2,1)S(1)}, u32[]{:S(2)}, u32[]{:S(2)}) collective-permute-start(bf16[2,512,640]{2,1,0:T(8,128)(2,1)S(1)} %fetch.1), channel_id=1, source_target_pairs={{0,8},{8,16},{16,24},{24,32},{32,40},{40,48},{48,56},{56,64},{64,7... | collective-permute-start | bytes 3932168 | tf_op jit(solution)/shard_map/ppermute | solution.py:543
  14.1 10.6 %collective-permute-start.1 = (bf16[4,240,640]{2,1,0:T(8,128)(2,1)S(1)}, bf16[4,240,640]{2,1,0:T(8,128)(2,1)S(1)}, u32[]{:S(2)}, u32[]{:S(2)}) collective-permute-start(bf16[4,240,640]{2,1,0:T(8,128)(2,1)S(1)} %get-tuple-element.31), channel_id=1, source_target_pairs={{0,8},{8,0},{16,24},{24,16},{32,40},{40,32},{48,56},{56,48},{64,72... | collective-permute-start | bytes 3686408 | tf_op jit(solution)/shard_map/ppermute | solution.py:543
  25.0 17.3 %collective-permute-start.4 = (bf16[240,640]{1,0:T(8,128)(2,1)S(1)}, bf16[240,640]{1,0:T(8,128)(2,1)S(1)}, u32[]{:S(2)}, u32[]{:S(2)}) collective-permute-start(bf16[240,640]{1,0:T(8,128)(2,1)S(1)} %get-tuple-element.62), channel_id=1, source_target_pairs={{0,48},{8,56},{16,0},{24,8},{32,16},{40,24},{48,32},{56,40},{64,11... | collective-permute-start | bytes 921608 | tf_op jit(solution)/shard_map/ppermute | solution.py:543
  29.0 13.3 %collective-permute-start.3 = (bf16[240,640]{1,0:T(8,128)(2,1)S(1)}, bf16[240,640]{1,0:T(8,128)(2,1)S(1)}, u32[]{:S(2)}, u32[]{:S(2)}) collective-permute-start(bf16[240,640]{1,0:T(8,128)(2,1)S(1)} %get-tuple-element.63), channel_id=1, source_target_pairs={{0,32},{8,40},{16,48},{24,56},{32,0},{40,8},{48,16},{56,24},{64,96... | collective-permute-start | bytes 921608 | tf_op jit(solution)/shard_map/ppermute | solution.py:543
  29.0 16.7 %collective-permute-start.2 = (bf16[240,640]{1,0:T(8,128)(2,1)S(1)}, bf16[240,640]{1,0:T(8,128)(2,1)S(1)}, u32[]{:S(2)}, u32[]{:S(2)}) collective-permute-start(bf16[240,640]{1,0:T(8,128)(2,1)S(1)} %get-tuple-element.64), channel_id=1, source_target_pairs={{0,16},{8,24},{16,32},{24,40},{32,48},{40,56},{48,0},{56,8},{64,80... | collective-permute-start | bytes 921608 | tf_op jit(solution)/shard_map/ppermute | solution.py:543
  46.6 12.2 %collective-permute-start.5 = (bf16[240,640]{1,0:T(8,128)(2,1)S(1)}, bf16[240,640]{1,0:T(8,128)(2,1)S(1)}, u32[]{:S(2)}, u32[]{:S(2)}) collective-permute-start(bf16[240,640]{1,0:T(8,128)(2,1)S(1)} %get-tuple-element.39), channel_id=1, source_target_pairs={{0,72},{8,64},{16,88},{24,80},{32,104},{40,96},{48,120},{56,112},{... | collective-permute-start | bytes 921608 | tf_op jit(solution)/shard_map/ppermute | solution.py:543
  58.9 10.2 %collective-permute-start.8 = (bf16[240,640]{1,0:T(8,128)(2,1)S(1)}, bf16[240,640]{1,0:T(8,128)(2,1)S(1)}, u32[]{:S(2)}, u32[]{:S(2)}) collective-permute-start(bf16[240,640]{1,0:T(8,128)(2,1)S(1)} %collective-permute-done.5.refs_0_), channel_id=1, source_target_pairs={{0,48},{8,56},{16,0},{24,8},{32,16},{40,24},{48,32},{56,40},{64,11... | collective-permute-start | bytes 921608 | tf_op jit(solution)/shard_map/ppermute | solution.py:543
  59.9 11.8 %collective-permute-start.7 = (bf16[240,640]{1,0:T(8,128)(2,1)S(1)}, bf16[240,640]{1,0:T(8,128)(2,1)S(1)}, u32[]{:S(2)}, u32[]{:S(2)}) collective-permute-start(bf16[240,640]{1,0:T(8,128)(2,1)S(1)} %collective-permute-done.5.refs_0_), channel_id=1, source_target_pairs={{0,32},{8,40},{16,48},{24,56},{32,0},{40,8},{48,16},{56,24},{64,96... | collective-permute-start | bytes 921608 | tf_op jit(solution)/shard_map/ppermute | solution.py:543
  60.1 15.9 %collective-permute-start.6 = (bf16[240,640]{1,0:T(8,128)(2,1)S(1)}, bf16[240,640]{1,0:T(8,128)(2,1)S(1)}, u32[]{:S(2)}, u32[]{:S(2)}) collective-permute-start(bf16[240,640]{1,0:T(8,128)(2,1)S(1)} %collective-permute-done.5.refs_0_), channel_id=1, source_target_pairs={{0,16},{8,24},{16,32},{24,40},{32,48},{40,56},{48,0},{56,8},{64,80... | collective-permute-start | bytes 921608 | tf_op jit(solution)/shard_map/ppermute | solution.py:543
  76.2 3.0 %collective-permute-start.9 = (bf16[4,240,640]{2,1,0:T(8,128)(2,1)S(1)}, bf16[4,240,640]{2,1,0:T(8,128)(2,1)S(1)}, u32[]{:S(2)}, u32[]{:S(2)}) collective-permute-start(bf16[4,240,640]{2,1,0:T(8,128)(2,1)S(1)} %pad_maximum_fusion), channel_id=1, source_target_pairs={{0,8},{8,0},{16,24},{24,16},{32,40},{40,32},{48,56},{56,48},{64,72... | collective-permute-start | bytes 3686408 | tf_op jit(solution)/shard_map/ppermute | solution.py:543
  77.5 3.4 %collective-permute-start.10 = (bf16[4,240,640]{2,1,0:T(8,128)(2,1)S(1)}, bf16[4,240,640]{2,1,0:T(8,128)(2,1)S(1)}, u32[]{:S(2)}, u32[]{:S(2)}) collective-permute-start(bf16[4,240,640]{2,1,0:T(8,128)(2,1)S(1)} %get-tuple-element.47), channel_id=1, source_target_pairs={{0,8},{8,0},{16,24},{24,16},{32,40},{40,32},{48,56},{56,48},{64,72... | collective-permute-start | bytes 3686408 | tf_op jit(solution)/shard_map/ppermute | solution.py:543
  80.9 5.8 %copy-start.1 = (bf16[2048,640]{1,0:T(8,128)(2,1)S(1)}, bf16[2048,640]{1,0:T(8,128)(2,1)}, u32[]{:S(2)}) copy-start(bf16[2048,640]{1,0:T(8,128)(2,1)} %q_ref.7) | copy-start | bytes 7864324
  80.9 5.8 %copy-start.2 = (f32[1,640]{1,0:T(1,128)S(1)}, f32[1,640]{1,0:T(1,128)}, u32[]{:S(2)}) copy-start(f32[1,640]{1,0:T(1,128)} %gain_ref.1) | copy-start | bytes 7684
  81.0 16.0 %collective-permute-start.13 = (bf16[240,640]{1,0:T(8,128)(2,1)S(1)}, bf16[240,640]{1,0:T(8,128)(2,1)S(1)}, u32[]{:S(2)}, u32[]{:S(2)}) collective-permute-start(bf16[240,640]{1,0:T(8,128)(2,1)S(1)} %fusion.3), channel_id=1, source_target_pairs={{0,32},{8,40},{16,48},{24,56},{32,0},{40,8},{48,16},{56,24},{64,96... | collective-permute-start | bytes 921608 | tf_op jit(solution)/shard_map/ppermute | solution.py:543
  82.1 15.0 %collective-permute-start.12 = (bf16[144,640]{1,0:T(8,128)(2,1)S(1)}, bf16[144,640]{1,0:T(8,128)(2,1)S(1)}, u32[]{:S(2)}, u32[]{:S(2)}) collective-permute-start(bf16[144,640]{1,0:T(8,128)(2,1)S(1)} %get-tuple-element.60), channel_id=1, source_target_pairs={{0,48},{8,56},{16,0},{24,8},{32,16},{40,24},{48,32},{56,40},{64,11... | collective-permute-start | bytes 552968 | tf_op jit(solution)/shard_map/ppermute | solution.py:543
  83.4 13.7 %collective-permute-start.11 = (bf16[144,640]{1,0:T(8,128)(2,1)S(1)}, bf16[144,640]{1,0:T(8,128)(2,1)S(1)}, u32[]{:S(2)}, u32[]{:S(2)}) collective-permute-start(bf16[144,640]{1,0:T(8,128)(2,1)S(1)} %get-tuple-element.61), channel_id=1, source_target_pairs={{0,16},{8,24},{16,32},{24,40},{32,48},{40,56},{48,0},{56,8},{64,80... | collective-permute-start | bytes 552968 | tf_op jit(solution)/shard_map/ppermute | solution.py:543
  84.3 14.2 %collective-permute-start.16 = (bf16[96,640]{1,0:T(8,128)(2,1)S(1)}, bf16[96,640]{1,0:T(8,128)(2,1)S(1)}, u32[]{:S(2)}, u32[]{:S(2)}) collective-permute-start(bf16[96,640]{1,0:T(8,128)(2,1)S(1)} %get-tuple-element.58), channel_id=1, source_target_pairs={{0,48},{8,56},{16,0},{24,8},{32,16},{40,24},{48,32},{56,40},{64,11... | collective-permute-start | bytes 368648 | tf_op jit(solution)/shard_map/ppermute | solution.py:543
  86.8 11.8 %collective-permute-start.15 = (bf16[96,640]{1,0:T(8,128)(2,1)S(1)}, bf16[96,640]{1,0:T(8,128)(2,1)S(1)}, u32[]{:S(2)}, u32[]{:S(2)}) collective-permute-start(bf16[96,640]{1,0:T(8,128)(2,1)S(1)} %get-tuple-element.59), channel_id=1, source_target_pairs={{0,16},{8,24},{16,32},{24,40},{32,48},{40,56},{48,0},{56,8},{64,80... | collective-permute-start | bytes 368648 | tf_op jit(solution)/shard_map/ppermute | solution.py:543
  97.2 18.1 %collective-permute-start.14 = (bf16[3,40,640]{2,1,0:T(8,128)(2,1)S(1)}, bf16[3,40,640]{2,1,0:T(8,128)(2,1)S(1)}, u32[]{:S(2)}, u32[]{:S(2)}) collective-permute-start(bf16[3,40,640]{2,1,0:T(8,128)(2,1)S(1)} %get-tuple-element.55), channel_id=1, source_target_pairs={{64,0},{72,8},{80,16},{88,24},{96,32},{104,40},{112,48},{120,56},{... | collective-permute-start | bytes 460808 | tf_op jit(solution)/shard_map/ppermute | solution.py:543

commit v3 on v2

--- a/solution.py
+++ b/solution.py
@@ -372,25 +372,26 @@
     fill_gathered([source_refs[0].at[d] for d in range(RING)], w_ref)
 
 
-def fast_apply(info, queries, weights, gain, attended, tile=512):
+def fast_apply(info, queries, weights, gain, attended, tiles, partly=None, tile=512):
     rows, width = queries.shape
-    stream = pl.BlockSpec((tile, width), lambda i, s: (i, 0))
-
-    def body(info_ref, q_ref, w_ref, gain_ref, att_ref, o_ref):
+    stream = pl.BlockSpec((tile, width), lambda i, s: (i + tiles[0], 0))
+    kept = [] if partly is None else [partly]
+
+    def body(info_ref, q_ref, w_ref, gain_ref, att_ref, *rest):
         q = q_ref[...]
         gate_pre = dot(q, w_ref[0], NT)
         up_pre = dot(q, w_ref[1], NT)
         sig = 0.5 * jnp.tanh(0.5 * gate_pre) + 0.5
         out = dot((gate_pre * sig * up_pre).astype(BF16), w_ref[2], NN)
         inverse_rms = lax.rsqrt(jnp.mean(out * out, axis=-1, keepdims=True) + EPSILON)
-        o_ref[...] = (att_ref[...] + out * inverse_rms * gain_ref[...]).astype(BF16)
+        rest[-1][...] = (att_ref[...] + out * inverse_rms * gain_ref[...]).astype(BF16)
 
     return pl.pallas_call(
         body,
         out_shape=jax.ShapeDtypeStruct((rows, width), BF16),
         grid_spec=pltpu.PrefetchScalarGridSpec(
             num_scalar_prefetch=1,
-            grid=(rows // tile,),
+            grid=(tiles[1] - tiles[0],),
             in_specs=[
                 stream,
                 pl.BlockSpec(
@@ -398,12 +399,17 @@
                 ),
                 pl.BlockSpec((1, width), lambda i, s: (0, 0)),
                 stream,
-            ],
+            ]
+            + [ANYWHERE for _ in kept],
             out_specs=stream,
         ),
+        input_output_aliases={5: 0} if kept else {},
+        cost_estimate=pl.CostEstimate(
+            flops=1_380_000_000, bytes_accessed=0, transcendentals=0
+        ),
         compiler_params=params(32),
-        name="fast_apply",
-    )(info, queries, weights, gain, attended)
+        name=f"fast_apply_{tiles[0]}",
+    )(info, queries, weights, gain, attended, *kept)
 
 
 def renormalize(previous, gradient):
@@ -510,7 +516,7 @@
             num_scalar_prefetch=1, grid=(1,), in_specs=[HERE] * 7, out_specs=HERE
         ),
         cost_estimate=pl.CostEstimate(
-            flops=40_000_000_000, bytes_accessed=100_000_000, transcendentals=0
+            flops=920_000_000, bytes_accessed=0, transcendentals=0
         ),
         compiler_params=params(16),
         name="final_far",
@@ -624,10 +630,11 @@
     ring_b = [send(part, along_z(d)) for part, d in zip(part_b, (1, 3))]
     both_there = send(both, along_z(2))
     ready = after(info, both, *part_a, *part_b)
-    mixed = fast_apply(ready, fast_query, weights, gain, attended)
+    mixed = fast_apply(ready, fast_query, weights, gain, attended, (0, 2))
     near, far = sum_call(after(mine, mixed), other, [*ring_a, both_there])
     near = send(near, BACK)
-    far_rows = final_far(after(info, far), mine, other, [*ring_b, both_there], beside, far)
+    mixed = fast_apply(after(info, far), fast_query, weights, gain, attended, (2, 4), mixed)
+    far_rows = final_far(after(info, mixed), mine, other, [*ring_b, both_there], beside, far)
     final = final_near(info, middle, near, far_rows)
     return mixed, jnp.transpose(final, (1, 0, 2))[None]
 

time: 117 us -> 117 us (level)
  waiting for transfers between devices: 41.5 us -> 39.7 us
  Pallas kernels: 55.3 us -> 56.7 us
    ppermute x17, waiting for transfers between devices: 41.5 us -> 39.7 us  [send(): return lax.ppermute(x, 'seq', pairs)]
    pallas_call x1 -> x2, Pallas kernels: 10.3 us -> 11.7 us  [fast_apply(): pl.pallas_call(body, out_shape=jax.ShapeDtypeStruct((rows, width), BF16),...]
  transfers between devices with their start and end apart: 17 -> 17, of which waited for: 8 -> 10; matrix products, arithmetic and copies ran while one was open for 0% -> 0% of each run, Pallas kernels for 44% -> 45%
where the time goes in v3:
time: 117 us; the launch traced here: 116 us
  Pallas kernels  56.7 us (48%)
  waiting for transfers between devices  39.7 us (34%)
  starting transfers between devices  17.8 us (15%)
    ppermute x17, waiting for transfers between devices, send(): return lax.ppermute(x, 'seq', pairs)  39.7 us
    pallas_call x4, Pallas kernels, gradient_call(): pl.pallas_call(body, out_shape=shapes, grid_spec=pltpu.PrefetchScalarGrid...  22.1 us
    ppermute x17, starting transfers between devices, send(): return lax.ppermute(x, 'seq', pairs)  17.8 us
    pallas_call x2, Pallas kernels, attention_rest(): pl.pallas_call(body, out_shape=jax.ShapeDtypeStruct((rows, width), F32),...  13.2 us
    pallas_call x2, Pallas kernels, fast_apply(): pl.pallas_call(body, out_shape=jax.ShapeDtypeStruct((rows, width), BF16),...  11.7 us
    pallas_call x1, Pallas kernels, attention_first(): pl.pallas_call(body, out_shape=jax.ShapeDtypeStruct((rows, width), F32),...  4.61 us
  transfers between devices with their start and end apart: 17, of which 10 were waited for; matrix products, arithmetic and copies ran while one was open for 0% of the time, Pallas kernels for 45%

profile of v3, /device:TPU:0, one launch (start us, length us, event | category | flops | bytes accessed | tf_op | source)
XLA Modules:
  0.0 116.4 jit_solution(15286176934344342991)
XLA Ops:
  0.8 2.1 %fetch.1 = bf16[2,512,640]{2,1,0:T(8,128)(2,1)S(1)} custom-call(s32[4]{0:T(128)S(1)} %pad_add_fusion.info_ref, bf16[2048,640]{1,0:T(8,128)(2,1)} %kc_ref.5, bf16[2048,640]{1,0:T(8,128)(2,1)} %vc_ref.5), custom_call_target="tpu_custom_call" | custom-call | tf_op jit(solution)/shard_map/fetch/pallas_call | solution.py:258
  3.5 10.5 %first_theirs.1 = (bf16[4,240,640]{2,1,0:T(8,128)(2,1)S(1)}, bf16[3,640,640]{2,1,0:T(8,128)(2,1)S(1)}, bf16[2,2048,640]{2,1,0:T(8,128)(2,1)S(1)}) custom-call(s32[4]{0:T(128)S(1)} %pad_add_fusion.info_ref, f32[3,640,640]{2,1,0:T(8,128)S(1)} %bitcast.31, bf16[2048,640]{1,0:T(8,128)(2,1)} %refs_1_.3, bf16[2048,640]{1,0:T(8,128)(2,1)} %refs_2_.1, ...), custom_call_target="tpu_custom_call" | custom-call | tf_op jit(solution)/shard_map/first_theirs/pallas_call | solution.py:340
  14.1 1.6 %collective-permute-start.1 = (bf16[4,240,640]{2,1,0:T(8,128)(2,1)S(1)}, bf16[4,240,640]{2,1,0:T(8,128)(2,1)S(1)}, u32[]{:S(2)}, u32[]{:S(2)}) collective-permute-start(bf16[4,240,640]{2,1,0:T(8,128)(2,1)S(1)} %get-tuple-element.32), channel_id=1, source_target_pairs={{0,8},{8,0},{16,24},{24,16},{32,40},{40,32},{48,56},{56,48},{64,72... | collective-permute-start | bytes 3686408 | tf_op jit(solution)/shard_map/ppermute | solution.py:549
  15.7 9.0 %first_mine.1 = (bf16[4,240,640]{2,1,0:T(8,128)(2,1)S(1)}, bf16[3,640,640]{2,1,0:T(8,128)(2,1)S(1)}) custom-call(s32[4]{0:T(128)S(1)} %pad_add_fusion.info_ref, f32[3,640,640]{2,1,0:T(8,128)S(1)} %bitcast.32, bf16[2,2048,640]{2,1,0:T(8,128)(2,1)S(1)} %get-tuple-element.34.refs_1_.refs_4_, f32[1,2048]{1,0:T(1,128)} %bitcast.41, ...), custom_call_target="tpu_custom_call", output_to_operand_aliasing={{1}: (4, {})} | custom-call | tf_op jit(solution)/shard_map/first_mine/pallas_call | solution.py:340
  25.0 4.0 %collective-permute-start.4 = (bf16[240,640]{1,0:T(8,128)(2,1)S(1)}, bf16[240,640]{1,0:T(8,128)(2,1)S(1)}, u32[]{:S(2)}, u32[]{:S(2)}) collective-permute-start(bf16[240,640]{1,0:T(8,128)(2,1)S(1)} %get-tuple-element.64), channel_id=1, source_target_pairs={{0,48},{8,56},{16,0},{24,8},{32,16},{40,24},{48,32},{56,40},{64,11... | collective-permute-start | bytes 921608 | tf_op jit(solution)/shard_map/ppermute | solution.py:549
  30.0 2.4 %attention_rest_1.1.rest_0_ = f32[2048,640]{1,0:T(8,128)S(1)} custom-call(s32[4]{0:T(128)S(1)} %pad_add_fusion.info_ref, bf16[2048,640]{1,0:T(8,128)(2,1)} %q_ref.7, bf16[2048,640]{1,0:T(8,128)(2,1)} %kc_ref.5, bf16[2048,640]{1,0:T(8,128)(2,1)} %kc_ref.5, bf16[2048,640]{1,0:T(8,128)(2,1)} %vc_ref.5, bf16[2048,640]{1,0:T(8,128)(2,1)} %vc_ref.5), custom_call_target="tpu_custom_call" | custom-call | tf_op jit(solution)/shard_map/attention_rest_1/pallas_call | solution.py:114
  32.5 9.8 %collective-permute-done.4.c_ref = bf16[240,640]{1,0:T(8,128)(2,1)S(1)} collective-permute-done((bf16[240,640]{1,0:T(8,128)(2,1)S(1)}, bf16[240,640]{1,0:T(8,128)(2,1)S(1)}, u32[]{:S(2)}, u32[]{:S(2)}) %collective-permute-start.4) | collective-permute-done | bytes 307232 | tf_op jit(solution)/shard_map/ppermute | solution.py:549
  42.3 3.4 %collective-permute-done.2.a_ref = bf16[240,640]{1,0:T(8,128)(2,1)S(1)} collective-permute-done((bf16[240,640]{1,0:T(8,128)(2,1)S(1)}, bf16[240,640]{1,0:T(8,128)(2,1)S(1)}, u32[]{:S(2)}, u32[]{:S(2)}) %collective-permute-start.2) | collective-permute-done | bytes 307232 | tf_op jit(solution)/shard_map/ppermute | solution.py:549
  46.6 1.5 %collective-permute-start.5 = (bf16[240,640]{1,0:T(8,128)(2,1)S(1)}, bf16[240,640]{1,0:T(8,128)(2,1)S(1)}, u32[]{:S(2)}, u32[]{:S(2)}) collective-permute-start(bf16[240,640]{1,0:T(8,128)(2,1)S(1)} %get-tuple-element.40), channel_id=1, source_target_pairs={{0,72},{8,64},{16,88},{24,80},{32,104},{40,96},{48,120},{56,112},{... | collective-permute-start | bytes 921608 | tf_op jit(solution)/shard_map/ppermute | solution.py:549
  48.1 10.7 %attention_rest_0.1._ = f32[2048,640]{1,0:T(8,128)S(1)} custom-call(s32[4]{0:T(128)S(1)} %pad_add_fusion.info_ref, bf16[2048,640]{1,0:T(8,128)(2,1)} %q_ref.7, bf16[2048,640]{1,0:T(8,128)(2,1)} %kc_ref.5, bf16[2048,640]{1,0:T(8,128)(2,1)} %kc_ref.5, bf16[2048,640]{1,0:T(8,128)(2,1)} %vc_ref.5, ...), custom_call_target="tpu_custom_call", output_to_operand_aliasing={{}: (6, {})} | custom-call | tf_op jit(solution)/shard_map/attention_rest_0/pallas_call | solution.py:114
  61.0 4.6 %attention_first.1.att_ref = f32[2048,640]{1,0:T(8,128)S(1)} custom-call(s32[4]{0:T(128)S(1)} %pad_add_fusion.info_ref, bf16[2048,640]{1,0:T(8,128)(2,1)} %q_ref.7, bf16[2,512,640]{2,1,0:T(8,128)(2,1)S(1)} %collective-permute-done.kp_ref.vp_ref, bf16[2048,640]{1,0:T(8,128)(2,1)} %kc_ref.5, ...), custom_call_target="tpu_custom_call", output_to_operand_aliasing={{}: (6, {})} | custom-call | tf_op jit(solution)/shard_map/attention_first/pallas_call | solution.py:79
  65.6 3.5 %collective-permute-done.8.refs_3_ = bf16[240,640]{1,0:T(8,128)(2,1)S(1)} collective-permute-done((bf16[240,640]{1,0:T(8,128)(2,1)S(1)}, bf16[240,640]{1,0:T(8,128)(2,1)S(1)}, u32[]{:S(2)}, u32[]{:S(2)}) %collective-permute-start.8) | collective-permute-done | bytes 307232 | tf_op jit(solution)/shard_map/ppermute | solution.py:549
  69.1 2.5 %collective-permute-done.7.refs_2_ = bf16[240,640]{1,0:T(8,128)(2,1)S(1)} collective-permute-done((bf16[240,640]{1,0:T(8,128)(2,1)S(1)}, bf16[240,640]{1,0:T(8,128)(2,1)S(1)}, u32[]{:S(2)}, u32[]{:S(2)}) %collective-permute-start.7) | collective-permute-done | bytes 307232 | tf_op jit(solution)/shard_map/ppermute | solution.py:549
  71.6 4.4 %collective-permute-done.6.refs_1_ = bf16[240,640]{1,0:T(8,128)(2,1)S(1)} collective-permute-done((bf16[240,640]{1,0:T(8,128)(2,1)S(1)}, bf16[240,640]{1,0:T(8,128)(2,1)S(1)}, u32[]{:S(2)}, u32[]{:S(2)}) %collective-permute-start.6) | collective-permute-done | bytes 307232 | tf_op jit(solution)/shard_map/ppermute | solution.py:549
  76.3 1.2 %second_theirs.1 = (bf16[4,240,640]{2,1,0:T(8,128)(2,1)S(1)}, bf16[3,640,640]{2,1,0:T(8,128)(2,1)S(1)}) custom-call(s32[4]{0:T(128)S(1)} %pad_add_fusion.info_ref, bf16[240,640]{1,0:T(8,128)(2,1)S(1)} %collective-permute-done.5.refs_0_, bf16[240,640]{1,0:T(8,128)(2,1)S(1)} %collective-permute-done.6.refs_1_, ...), custom_call_target="tpu_custom_call", output_to_operand_aliasing={{1}: (7, {})} | custom-call | tf_op jit(solution)/shard_map/second_theirs/pallas_call | solution.py:340
  79.2 1.2 %second_mine.1 = (bf16[4,240,640]{2,1,0:T(8,128)(2,1)S(1)}, bf16[3,640,640]{2,1,0:T(8,128)(2,1)S(1)}) custom-call(s32[4]{0:T(128)S(1)} %pad_add_fusion.info_ref, bf16[4,240,640]{2,1,0:T(8,128)(2,1)S(1)} %collective-permute-done.9.refs_0_.cast_ref, bf16[2,2048,640]{2,1,0:T(8,128)(2,1)S(1)} %get-tuple-element.34.refs_1_.refs_4_, ...), custom_call_target="tpu_custom_call", output_to_operand_aliasing={{1}: (4, {})} | custom-call | tf_op jit(solution)/shard_map/second_mine/pallas_call | solution.py:340
  82.1 1.3 %collective-permute-start.12 = (bf16[144,640]{1,0:T(8,128)(2,1)S(1)}, bf16[144,640]{1,0:T(8,128)(2,1)S(1)}, u32[]{:S(2)}, u32[]{:S(2)}) collective-permute-start(bf16[144,640]{1,0:T(8,128)(2,1)S(1)} %get-tuple-element.62), channel_id=1, source_target_pairs={{0,48},{8,56},{16,0},{24,8},{32,16},{40,24},{48,32},{56,40},{64,11... | collective-permute-start | bytes 552968 | tf_op jit(solution)/shard_map/ppermute | solution.py:549
  84.3 2.5 %collective-permute-start.16 = (bf16[96,640]{1,0:T(8,128)(2,1)S(1)}, bf16[96,640]{1,0:T(8,128)(2,1)S(1)}, u32[]{:S(2)}, u32[]{:S(2)}) collective-permute-start(bf16[96,640]{1,0:T(8,128)(2,1)S(1)} %get-tuple-element.60), channel_id=1, source_target_pairs={{0,48},{8,56},{16,0},{24,8},{32,16},{40,24},{48,32},{56,40},{64,11... | collective-permute-start | bytes 368648 | tf_op jit(solution)/shard_map/ppermute | solution.py:549
  86.8 5.9 %fast_apply_0.1.rest_0_ = bf16[2048,640]{1,0:T(8,128)(2,1)} custom-call(s32[4]{0:T(128)S(1)} %pad_add_fusion.info_ref, bf16[2048,640]{1,0:T(8,128)(2,1)S(1)} %copy-done.1, bf16[3,640,640]{2,1,0:T(8,128)(2,1)S(1)} %get-tuple-element.53.w_ref, f32[1,640]{1,0:T(1,128)S(1)} %copy-done.2, f32[2048,640]{1,0:T(8,128)S(1)} %attention_first.1.att_ref), custom_call_target="tpu_custom_call" | custom-call | flops 1380000000 | tf_op jit(solution)/shard_map/fast_apply_0/pallas_call | solution.py:389
  92.6 2.5 %collective-permute-done.12.b_ref = bf16[144,640]{1,0:T(8,128)(2,1)S(1)} collective-permute-done((bf16[144,640]{1,0:T(8,128)(2,1)S(1)}, bf16[144,640]{1,0:T(8,128)(2,1)S(1)}, u32[]{:S(2)}, u32[]{:S(2)}) %collective-permute-start.12) | collective-permute-done | bytes 184352 | tf_op jit(solution)/shard_map/ppermute | solution.py:549
  96.1 1.3 %collective-permute-start.14 = (bf16[3,40,640]{2,1,0:T(8,128)(2,1)S(1)}, bf16[3,40,640]{2,1,0:T(8,128)(2,1)S(1)}, u32[]{:S(2)}, u32[]{:S(2)}) collective-permute-start(bf16[3,40,640]{2,1,0:T(8,128)(2,1)S(1)} %get-tuple-element.58), channel_id=1, source_target_pairs={{64,0},{72,8},{80,16},{88,24},{96,32},{104,40},{112,48},{120,56},{... | collective-permute-start | bytes 460808 | tf_op jit(solution)/shard_map/ppermute | solution.py:549
  97.4 5.9 %fast_apply_2.1 = bf16[2048,640]{1,0:T(8,128)(2,1)} custom-call(s32[4]{0:T(128)S(1)} %pad_add_fusion.info_ref, bf16[2048,640]{1,0:T(8,128)(2,1)S(1)} %copy-done.1, bf16[3,640,640]{2,1,0:T(8,128)(2,1)S(1)} %get-tuple-element.53.w_ref, f32[1,640]{1,0:T(1,128)S(1)} %copy-done.2, ...), custom_call_target="tpu_custom_call", output_to_operand_aliasing={{}: (5, {})} | custom-call | flops 1380000000 | tf_op jit(solution)/shard_map/fast_apply_2/pallas_call | solution.py:389
  103.8 11.2 %collective-permute-done.14.near_ref = bf16[3,40,640]{2,1,0:T(8,128)(2,1)S(1)} collective-permute-done((bf16[3,40,640]{2,1,0:T(8,128)(2,1)S(1)}, bf16[3,40,640]{2,1,0:T(8,128)(2,1)S(1)}, u32[]{:S(2)}, u32[]{:S(2)}) %collective-permute-start.14) | collective-permute-done | bytes 153632 | tf_op jit(solution)/shard_map/ppermute | solution.py:549
  115.0 1.4 %final_near.1 = f32[3,40,640]{2,1,0:T(8,128)} custom-call(s32[4]{0:T(128)S(1)} %pad_add_fusion.info_ref, f32[3,40,640]{2,1,0:T(8,128)S(1)} %get-tuple-element.57.middle_ref, bf16[3,40,640]{2,1,0:T(8,128)(2,1)S(1)} %collective-permute-done.14.near_ref, f32[3,40,640]{2,1,0:T(8,128)S(1)} %final_far.1.far_ref), custom_call_target="tpu_custom_call" | custom-call | tf_op jit(solution)/shard_map/final_near/pallas_call | solution.py:537
  (36 shorter events, 11.1 us)
Async XLA Ops:
  0.8 2.8 %copy-start = (f32[1,640,3,640]{3,1,2,0:T(8,128)S(1)}, f32[1,640,3,640]{3,1,2,0:T(8,128)}, u32[]{:S(2)}) copy-start(f32[1,640,3,640]{3,1,2,0:T(8,128)} %param.16) | copy-start | bytes 14745604
  2.9 21.8 %collective-permute-start = (bf16[2,512,640]{2,1,0:T(8,128)(2,1)S(1)}, bf16[2,512,640]{2,1,0:T(8,128)(2,1)S(1)}, u32[]{:S(2)}, u32[]{:S(2)}) collective-permute-start(bf16[2,512,640]{2,1,0:T(8,128)(2,1)S(1)} %fetch.1), channel_id=1, source_target_pairs={{0,8},{8,16},{16,24},{24,32},{32,40},{40,48},{48,56},{56,64},{64,7... | collective-permute-start | bytes 3932168 | tf_op jit(solution)/shard_map/ppermute | solution.py:549
  14.1 10.6 %collective-permute-start.1 = (bf16[4,240,640]{2,1,0:T(8,128)(2,1)S(1)}, bf16[4,240,640]{2,1,0:T(8,128)(2,1)S(1)}, u32[]{:S(2)}, u32[]{:S(2)}) collective-permute-start(bf16[4,240,640]{2,1,0:T(8,128)(2,1)S(1)} %get-tuple-element.32), channel_id=1, source_target_pairs={{0,8},{8,0},{16,24},{24,16},{32,40},{40,32},{48,56},{56,48},{64,72... | collective-permute-start | bytes 3686408 | tf_op jit(solution)/shard_map/ppermute | solution.py:549
  25.0 17.3 %collective-permute-start.4 = (bf16[240,640]{1,0:T(8,128)(2,1)S(1)}, bf16[240,640]{1,0:T(8,128)(2,1)S(1)}, u32[]{:S(2)}, u32[]{:S(2)}) collective-permute-start(bf16[240,640]{1,0:T(8,128)(2,1)S(1)} %get-tuple-element.64), channel_id=1, source_target_pairs={{0,48},{8,56},{16,0},{24,8},{32,16},{40,24},{48,32},{56,40},{64,11... | collective-permute-start | bytes 921608 | tf_op jit(solution)/shard_map/ppermute | solution.py:549
  29.0 13.3 %collective-permute-start.3 = (bf16[240,640]{1,0:T(8,128)(2,1)S(1)}, bf16[240,640]{1,0:T(8,128)(2,1)S(1)}, u32[]{:S(2)}, u32[]{:S(2)}) collective-permute-start(bf16[240,640]{1,0:T(8,128)(2,1)S(1)} %get-tuple-element.65), channel_id=1, source_target_pairs={{0,32},{8,40},{16,48},{24,56},{32,0},{40,8},{48,16},{56,24},{64,96... | collective-permute-start | bytes 921608 | tf_op jit(solution)/shard_map/ppermute | solution.py:549
  29.0 16.7 %collective-permute-start.2 = (bf16[240,640]{1,0:T(8,128)(2,1)S(1)}, bf16[240,640]{1,0:T(8,128)(2,1)S(1)}, u32[]{:S(2)}, u32[]{:S(2)}) collective-permute-start(bf16[240,640]{1,0:T(8,128)(2,1)S(1)} %get-tuple-element.66), channel_id=1, source_target_pairs={{0,16},{8,24},{16,32},{24,40},{32,48},{40,56},{48,0},{56,8},{64,80... | collective-permute-start | bytes 921608 | tf_op jit(solution)/shard_map/ppermute | solution.py:549
  46.6 12.2 %collective-permute-start.5 = (bf16[240,640]{1,0:T(8,128)(2,1)S(1)}, bf16[240,640]{1,0:T(8,128)(2,1)S(1)}, u32[]{:S(2)}, u32[]{:S(2)}) collective-permute-start(bf16[240,640]{1,0:T(8,128)(2,1)S(1)} %get-tuple-element.40), channel_id=1, source_target_pairs={{0,72},{8,64},{16,88},{24,80},{32,104},{40,96},{48,120},{56,112},{... | collective-permute-start | bytes 921608 | tf_op jit(solution)/shard_map/ppermute | solution.py:549
  58.9 10.2 %collective-permute-start.8 = (bf16[240,640]{1,0:T(8,128)(2,1)S(1)}, bf16[240,640]{1,0:T(8,128)(2,1)S(1)}, u32[]{:S(2)}, u32[]{:S(2)}) collective-permute-start(bf16[240,640]{1,0:T(8,128)(2,1)S(1)} %collective-permute-done.5.refs_0_), channel_id=1, source_target_pairs={{0,48},{8,56},{16,0},{24,8},{32,16},{40,24},{48,32},{56,40},{64,11... | collective-permute-start | bytes 921608 | tf_op jit(solution)/shard_map/ppermute | solution.py:549
  59.9 11.8 %collective-permute-start.7 = (bf16[240,640]{1,0:T(8,128)(2,1)S(1)}, bf16[240,640]{1,0:T(8,128)(2,1)S(1)}, u32[]{:S(2)}, u32[]{:S(2)}) collective-permute-start(bf16[240,640]{1,0:T(8,128)(2,1)S(1)} %collective-permute-done.5.refs_0_), channel_id=1, source_target_pairs={{0,32},{8,40},{16,48},{24,56},{32,0},{40,8},{48,16},{56,24},{64,96... | collective-permute-start | bytes 921608 | tf_op jit(solution)/shard_map/ppermute | solution.py:549
  60.1 15.9 %collective-permute-start.6 = (bf16[240,640]{1,0:T(8,128)(2,1)S(1)}, bf16[240,640]{1,0:T(8,128)(2,1)S(1)}, u32[]{:S(2)}, u32[]{:S(2)}) collective-permute-start(bf16[240,640]{1,0:T(8,128)(2,1)S(1)} %collective-permute-done.5.refs_0_), channel_id=1, source_target_pairs={{0,16},{8,24},{16,32},{24,40},{32,48},{40,56},{48,0},{56,8},{64,80... | collective-permute-start | bytes 921608 | tf_op jit(solution)/shard_map/ppermute | solution.py:549
  76.2 3.0 %collective-permute-start.9 = (bf16[4,240,640]{2,1,0:T(8,128)(2,1)S(1)}, bf16[4,240,640]{2,1,0:T(8,128)(2,1)S(1)}, u32[]{:S(2)}, u32[]{:S(2)}) collective-permute-start(bf16[4,240,640]{2,1,0:T(8,128)(2,1)S(1)} %pad_maximum_fusion), channel_id=1, source_target_pairs={{0,8},{8,0},{16,24},{24,16},{32,40},{40,32},{48,56},{56,48},{64,72... | collective-permute-start | bytes 3686408 | tf_op jit(solution)/shard_map/ppermute | solution.py:549
  77.5 3.4 %collective-permute-start.10 = (bf16[4,240,640]{2,1,0:T(8,128)(2,1)S(1)}, bf16[4,240,640]{2,1,0:T(8,128)(2,1)S(1)}, u32[]{:S(2)}, u32[]{:S(2)}) collective-permute-start(bf16[4,240,640]{2,1,0:T(8,128)(2,1)S(1)} %get-tuple-element.48), channel_id=1, source_target_pairs={{0,8},{8,0},{16,24},{24,16},{32,40},{40,32},{48,56},{56,48},{64,72... | collective-permute-start | bytes 3686408 | tf_op jit(solution)/shard_map/ppermute | solution.py:549
  80.9 5.8 %copy-start.1 = (bf16[2048,640]{1,0:T(8,128)(2,1)S(1)}, bf16[2048,640]{1,0:T(8,128)(2,1)}, u32[]{:S(2)}) copy-start(bf16[2048,640]{1,0:T(8,128)(2,1)} %q_ref.9) | copy-start | bytes 7864324
  80.9 5.8 %copy-start.2 = (f32[1,640]{1,0:T(1,128)S(1)}, f32[1,640]{1,0:T(1,128)}, u32[]{:S(2)}) copy-start(f32[1,640]{1,0:T(1,128)} %gain_ref.3) | copy-start | bytes 7684
  81.0 14.9 %collective-permute-start.13 = (bf16[240,640]{1,0:T(8,128)(2,1)S(1)}, bf16[240,640]{1,0:T(8,128)(2,1)S(1)}, u32[]{:S(2)}, u32[]{:S(2)}) collective-permute-start(bf16[240,640]{1,0:T(8,128)(2,1)S(1)} %fusion.3), channel_id=1, source_target_pairs={{0,32},{8,40},{16,48},{24,56},{32,0},{40,8},{48,16},{56,24},{64,96... | collective-permute-start | bytes 921608 | tf_op jit(solution)/shard_map/ppermute | solution.py:549
  82.1 13.0 %collective-permute-start.12 = (bf16[144,640]{1,0:T(8,128)(2,1)S(1)}, bf16[144,640]{1,0:T(8,128)(2,1)S(1)}, u32[]{:S(2)}, u32[]{:S(2)}) collective-permute-start(bf16[144,640]{1,0:T(8,128)(2,1)S(1)} %get-tuple-element.62), channel_id=1, source_target_pairs={{0,48},{8,56},{16,0},{24,8},{32,16},{40,24},{48,32},{56,40},{64,11... | collective-permute-start | bytes 552968 | tf_op jit(solution)/shard_map/ppermute | solution.py:549
  83.4 12.6 %collective-permute-start.11 = (bf16[144,640]{1,0:T(8,128)(2,1)S(1)}, bf16[144,640]{1,0:T(8,128)(2,1)S(1)}, u32[]{:S(2)}, u32[]{:S(2)}) collective-permute-start(bf16[144,640]{1,0:T(8,128)(2,1)S(1)} %get-tuple-element.63), channel_id=1, source_target_pairs={{0,16},{8,24},{16,32},{24,40},{32,48},{40,56},{48,0},{56,8},{64,80... | collective-permute-start | bytes 552968 | tf_op jit(solution)/shard_map/ppermute | solution.py:549
  84.3 19.0 %collective-permute-start.16 = (bf16[96,640]{1,0:T(8,128)(2,1)S(1)}, bf16[96,640]{1,0:T(8,128)(2,1)S(1)}, u32[]{:S(2)}, u32[]{:S(2)}) collective-permute-start(bf16[96,640]{1,0:T(8,128)(2,1)S(1)} %get-tuple-element.60), channel_id=1, source_target_pairs={{0,48},{8,56},{16,0},{24,8},{32,16},{40,24},{48,32},{56,40},{64,11... | collective-permute-start | bytes 368648 | tf_op jit(solution)/shard_map/ppermute | solution.py:549
  86.8 16.5 %collective-permute-start.15 = (bf16[96,640]{1,0:T(8,128)(2,1)S(1)}, bf16[96,640]{1,0:T(8,128)(2,1)S(1)}, u32[]{:S(2)}, u32[]{:S(2)}) collective-permute-start(bf16[96,640]{1,0:T(8,128)(2,1)S(1)} %get-tuple-element.61), channel_id=1, source_target_pairs={{0,16},{8,24},{16,32},{24,40},{32,48},{40,56},{48,0},{56,8},{64,80... | collective-permute-start | bytes 368648 | tf_op jit(solution)/shard_map/ppermute | solution.py:549
  96.1 18.9 %collective-permute-start.14 = (bf16[3,40,640]{2,1,0:T(8,128)(2,1)S(1)}, bf16[3,40,640]{2,1,0:T(8,128)(2,1)S(1)}, u32[]{:S(2)}, u32[]{:S(2)}) collective-permute-start(bf16[3,40,640]{2,1,0:T(8,128)(2,1)S(1)} %get-tuple-element.58), channel_id=1, source_target_pairs={{64,0},{72,8},{80,16},{88,24},{96,32},{104,40},{112,48},{120,56},{... | collective-permute-start | bytes 460808 | tf_op jit(solution)/shard_map/ppermute | solution.py:549
